TPU v7x, 256 devices: a whole 4x4x8 slice. The times are simulated.
256 devices in a mesh: expert: 16 (over y, x), tensor: 16 (over z, core).
Axes of the slice: x: 4, y: 4, z: 8, core: 2. Of those that a mesh axis runs over, the one named last changes fastest.
Arguments:
- queries: bfloat16 [4096, 8192], P('expert', 'tensor'), may hold values from -8 to 8
- keys_values: bfloat16 [16, 4, 1280, 256], P('expert'), may hold values from -6 to 6
- prefix_len: int32 [16], P('expert'), may hold values from 128 to 1024, as said below
- out_proj: bfloat16 [8192, 4096], P('tensor', 'expert'), may hold values from -0.0625 to 0.0625
- residual: bfloat16 [4096, 4096], P(('expert', 'tensor')), may hold values from -1.796875 to 1.796875
- norm_gain: float32 [4096], replicated, may hold values from 0.1 to 1.9
- expert_ids: int32 [4096, 8], P('expert'), may hold values from 0 to 63, all different within a row; in each aligned block of 16 rows (0 to 15, 16 to 31, ...) at most 3 rows name the same one
- route_weights: bfloat16 [4096, 8], P('expert'), may hold values from 0.19921875 to 1
- w_gate: bfloat16 [256, 4096, 384], P(('expert', 'tensor')), may hold values from -0.09375 to 0.09375
- w_up: bfloat16 [256, 4096, 384], P(('expert', 'tensor')), may hold values from -0.09375 to 0.09375
- w_down: bfloat16 [256, 384, 4096], P(('expert', 'tensor')), may hold values from -0.15625 to 0.15625
Outputs:
- layer_out: bfloat16 [4096, 4096], P(('expert', 'tensor'))
Inputs may be any that keep to these rules, and one draw needn't show every extreme that they name: `expert_ids`: in the rows of one device (aligned blocks of 16 rows) no expert is named by more than 3 rows, a bound that some block reaches; a row names 8 different experts. `prefix_len`: some sequence has all 1024 slots live.
All inputs are finite; a program needn't handle non-finite values.
Results may differ from a plain program's by a relative error of at most 0.035.
Values may be sent and summed in bfloat16 or wider, within the bound.
No kernel may reach another device: no remote copies, remote signals or barrier semaphores. Data moves between devices by JAX's collectives and lax.ppermute only.
A program may use at most 128 MiB of HBM per device.

v0:
```python
import math

import jax
import jax.numpy as jnp
from jax import lax
from jax.sharding import PartitionSpec as P

HEADS = 64
KVH = 4
HD = 128
TOPK = 8
HSPLIT = 4
TOK_DEV = 16
PREFIX = 1024


def norm_rows(hidden_state, norm_gain):
    values = hidden_state.astype(jnp.float32)
    factor = lax.rsqrt(jnp.mean(values * values, axis=-1, keepdims=True) + 1e-06)
    return (values * factor * norm_gain[None, :]).astype(jnp.bfloat16)


def route_tables(expert_ids, route_weights, experts, most_rows):
    total_rows = expert_ids.shape[0]
    named_mask = expert_ids[:, :, None] == jnp.arange(experts, dtype=jnp.int32)[None, None, :]
    hit_table = jnp.sum(named_mask.astype(jnp.int32), axis=1)
    weight_table = jnp.sum(
        jnp.where(named_mask, route_weights[:, :, None].astype(jnp.float32), 0.0), axis=1
    )
    grouped = hit_table.reshape(total_rows // TOK_DEV, TOK_DEV, experts)
    rank_table = (jnp.cumsum(grouped, axis=1) - grouped).reshape(total_rows, experts)
    share_index = (jnp.arange(total_rows, dtype=jnp.int32) // TOK_DEV)[:, None]
    position_table = share_index * most_rows + rank_table
    return (hit_table, weight_table, rank_table, position_table)


def pick_slot(table, expert_count, slot_count, slot_index):
    shaped = table.reshape(table.shape[0], expert_count, slot_count)
    return lax.dynamic_index_in_dim(shaped, slot_index, 2, keepdims=False)


def shards(
    queries,
    keys_values,
    prefix_len,
    out_proj,
    residual,
    norm_gain,
    expert_ids,
    route_weights,
    w_gate,
    w_up,
    w_down,
):
    tensor_count = lax.axis_size("tensor")
    expert_count = lax.axis_size("expert")
    tensor_index = lax.axis_index("tensor")
    step_rows = queries.shape[0]
    per_device = queries.shape[1] // HD
    group_size = HEADS // KVH
    kv_index = tensor_index * per_device // group_size
    cached = lax.dynamic_index_in_dim(keys_values[0], kv_index, 0, keepdims=False)
    key_rows = cached[:, :HD]
    value_rows = cached[:, HD:]
    context = cached.shape[0]
    query_rows = queries.reshape(step_rows, per_device, HD)
    scores = jnp.einsum(
        "nhd,cd->hnc", query_rows, key_rows, preferred_element_type=jnp.float32
    ) / math.sqrt(HD)
    columns = jnp.arange(context, dtype=jnp.int32)[None, :]
    positions = jnp.arange(step_rows, dtype=jnp.int32)[:, None]
    visible = ((columns < prefix_len[0]) | (columns >= PREFIX) & (columns - PREFIX <= positions))[
        None
    ]
    highest = jnp.max(jnp.where(visible, scores, -1e30), axis=-1, keepdims=True)
    weights = jnp.exp(jnp.where(visible, scores - highest, -1e30))
    summed = jnp.sum(weights, axis=-1)
    blended = jnp.einsum(
        "hnc,cd->nhd", weights.astype(jnp.bfloat16), value_rows, preferred_element_type=jnp.float32
    )
    attended = (
        (blended / jnp.transpose(summed)[:, :, None])
        .astype(jnp.bfloat16)
        .reshape(step_rows, per_device * HD)
    )
    head_part = jnp.dot(
        attended,
        lax.all_gather(out_proj, "expert", axis=1, tiled=True),
        preferred_element_type=jnp.float32,
    )
    slot_count = tensor_count // HSPLIT
    experts = expert_count * slot_count
    most_rows = min(TOK_DEV, max(2, TOK_DEV * TOPK // experts + 1))
    capacity = tensor_count * most_rows
    slot_index = tensor_index // HSPLIT
    start_row = tensor_index * TOK_DEV
    hit_table, weight_table, rank_table, position_table = route_tables(
        expert_ids, route_weights, experts, most_rows
    )
    hit_slot = pick_slot(hit_table, expert_count, slot_count, slot_index)
    weight_slot = pick_slot(weight_table, expert_count, slot_count, slot_index)
    position_slot = pick_slot(position_table, expert_count, slot_count, slot_index)
    slot_match = (hit_slot[:, :, None] == 1) & (
        position_slot[:, :, None] == jnp.arange(capacity, dtype=jnp.int32)[None, None, :]
    )
    head_sum = lax.psum(head_part.astype(jnp.bfloat16), "tensor").astype(jnp.float32)
    residual_full = lax.all_gather(residual, "tensor", axis=0, tiled=True)
    state_full = (residual_full.astype(jnp.float32) + head_sum).astype(jnp.bfloat16)
    hidden_state = lax.dynamic_slice_in_dim(state_full, start_row, TOK_DEV, 0)
    normed_full = norm_rows(state_full, norm_gain)
    source_rows = jnp.sum(
        jnp.where(slot_match, jnp.arange(step_rows, dtype=jnp.int32)[:, None, None], 0), axis=0
    )
    filled = jnp.any(slot_match, axis=0)
    outgoing = jnp.where(
        filled[:, :, None], jnp.take(normed_full, source_rows, axis=0), jnp.zeros((), jnp.bfloat16)
    )
    arrived_rows = lax.all_to_all(outgoing, "expert", split_axis=0, concat_axis=0, tiled=True)
    flat_rows = arrived_rows.reshape(-1, arrived_rows.shape[-1])
    gate_val = jnp.dot(flat_rows, w_gate[0], preferred_element_type=jnp.float32)
    up_val = jnp.dot(flat_rows, w_up[0], preferred_element_type=jnp.float32)
    inner = (jax.nn.silu(gate_val) * up_val).astype(jnp.bfloat16)
    result = jnp.dot(inner, w_down[0], preferred_element_type=jnp.float32).astype(jnp.bfloat16)
    computed = result.reshape(arrived_rows.shape)
    returned = lax.all_to_all(computed, "expert", split_axis=0, concat_axis=0, tiled=True)
    combine_weights = jnp.where(slot_match, weight_slot[:, :, None], 0.0).astype(jnp.bfloat16)
    expert_part = jnp.einsum(
        "njc,jcd->nd", combine_weights, returned, preferred_element_type=jnp.float32
    )
    expert_share = lax.psum_scatter(
        expert_part.astype(jnp.bfloat16), "tensor", scatter_dimension=0, tiled=True
    ).astype(jnp.float32)
    return (hidden_state.astype(jnp.float32) + expert_share).astype(jnp.bfloat16)


def solution(mesh):
    return jax.shard_map(
        shards,
        mesh=mesh,
        in_specs=(
            P("expert", "tensor"),
            P("expert", None, None, None),
            P("expert"),
            P("tensor", "expert"),
            P(("expert", "tensor"), None),
            P(),
            P("expert", None),
            P("expert", None),
            P(("expert", "tensor"), None, None),
            P(("expert", "tensor"), None, None),
            P(("expert", "tensor"), None, None),
        ),
        out_specs=P(("expert", "tensor"), None),
        check_vma=False,
    )
```

profile of v0, /device:TPU:2, one launch (start us, length us, event | category | flops | bytes accessed | tf_op | source)
XLA Modules:
  0.0 520.2 jit_solution(15658658182001831944)
XLA Ops:
  9.7 1.1 copy.38
  10.7 1.9 reduce_window_sum.14
  12.7 2.0 dynamic-slice_bitcast_fusion
  14.7 1.0 fusion.26
  15.7 5.1 fusion.62
  20.8 2.4 fusion.33
  23.2 51.8 %all-gather.5.cloned.1.call-done = bf16[512,4096]{1,0:T(8,128)(2,1)} async-done(((bf16[512,256]{1,0:T(8,128)(2,1)}), bf16[512,4096]{1,0:T(8,128)(2,1)}) %all-gather.5.cloned.1.call-update) | async-done | bytes 4194320 | tf_op jit(solution)/shard_map/all_gather | solution.py:88
  75.0 4.8 convolution_convert_fusion.1
  81.6 34.7 %all-gather.3.cloned.1.call-done = bf16[256,4096]{1,0:T(8,128)(2,1)} async-done(((bf16[16,4096]{1,0:T(8,128)(2,1)}), bf16[256,4096]{1,0:T(8,128)(2,1)}) %all-gather.3.cloned.1.call-update) | async-done | bytes 2097168 | tf_op jit(solution)/shard_map/all_gather | solution.py:107
  116.4 115.7 %all-reduce.2.cloned.1.call-done = bf16[256,4096]{1,0:T(8,128)(2,1)} async-done(((bf16[256,4096]{1,0:T(8,128)(2,1)}), bf16[256,4096]{1,0:T(8,128)(2,1)}) %all-reduce.2.cloned.1.call-update) | async-done | bytes 2097168 | tf_op jit(solution)/shard_map/psum | solution.py:106
  232.1 3.2 fusion.6
  235.3 1.3 copy-done.1
  236.6 2.0 fusion.8
  238.6 13.8 %gather_fusion = bf16[768,4096]{1,0:T(8,128)(2,1)} fusion(bf16[256,4096]{1,0:T(8,128)(2,1)} %fusion.8, s32[1024]{0:T(1024)S(1)} %pad_clamp_fusion), kind=kCustom, calls=%fused_computation | custom fusion | bytes 12585984 | tf_op jit(solution)/shard_map/jit(_take)/gather | solution.py:116
  252.4 3.9 select_select_fusion
  256.3 79.0 %all_to_all.10 = bf16[16,48,4096]{2,1,0:T(8,128)(2,1)S(1)} all-to-all(bf16[16,48,4096]{2,1,0:T(8,128)(2,1)S(1)} %select_select_fusion), channel_id=1, replica_groups=mesh['expert'=16,'tensor'=16] {'expert'}, dimensions={0} | all-to-all | bytes 12582912 | tf_op jit(solution)/shard_map/all_to_all | solution.py:118
  335.3 3.4 fusion.12
  338.7 3.5 fusion.22
  342.2 5.4 %convolution_convert_fusion = bf16[768,4096]{1,0:T(8,128)(2,1)} fusion(bf16[768,384]{1,0:T(8,128)(2,1)S(1)} %fusion.22, bf16[1,384,4096]{2,1,0:T(8,128)(2,1)S(1)} %copy-done), kind=kOutput, calls=%fused_computation.2 | convolution fusion | flops 2419064832 | bytes 10027008 | tf_op jit(solution)/shard_map/dot_general | solution.py:123
  347.6 6.0 %all-to-all-start.1 = ((bf16[16,48,4096]{2,1,0:T(8,128)(2,1)}), bf16[16,48,4096]{2,1,0:T(8,128)(2,1)}, u32[]{:S(2)}, u32[]{:S(2)}) async-start(bf16[16,48,4096]{2,1,0:T(8,128)(2,1)} %bitcast.108), calls=%async_computation.1 | async-start | bytes 12582912 | tf_op jit(solution)/shard_map/all_to_all | solution.py:125
  353.8 87.2 %all-to-all-done.1 = bf16[16,48,4096]{2,1,0:T(8,128)(2,1)} async-done(((bf16[16,48,4096]{2,1,0:T(8,128)(2,1)}), bf16[16,48,4096]{2,1,0:T(8,128)(2,1)}, u32[]{:S(2)}, u32[]{:S(2)}) %all-to-all-start.1) | async-done | bytes 6291488 | tf_op jit(solution)/shard_map/all_to_all | solution.py:125
  441.0 6.0 %fusion.3 = bf16[256,4096]{1,0:T(8,128)(2,1)} fusion(bf16[16,48,4096]{2,1,0:T(8,128)(2,1)} %all-to-all-done.1, bf16[256,16]{0,1:T(8,128)(2,1)S(1)} %bitcast.119, s32[256,16]{0,1:T(8,128)S(1)} %bitcast.113, pred[256,16]{0,1:T(8,128)(4,1)S(1)} %bitcast.118), kind=kOutput, calls=%fused_computation.11 | convolution fusion | flops 1612251136 | bytes 8417280 | tf_op jit(solution)/shard_map/njc,jcd->nd/dot_general | solution.py:127
  447.0 65.0 %reduce-scatter.2.cloned.1.call-done = bf16[16,4096]{1,0:T(8,128)(2,1)} async-done(((bf16[256,4096]{1,0:T(8,128)(2,1)}), bf16[16,4096]{1,0:T(8,128)(2,1)}) %reduce-scatter.2.cloned.1.call-update) | async-done | bytes 131088 | tf_op jit(solution)/shard_map/reduce_scatter | solution.py:130
  512.0 1.7 add_convert_fusion.1
  (44 shorter events, 4.4 us)
Async XLA Ops:
  6.5 335.7 %copy-start = (bf16[1,384,4096]{2,1,0:T(8,128)(2,1)S(1)}, bf16[1,384,4096]{2,1,0:T(8,128)(2,1)}, u32[]{:S(2)}) copy-start(bf16[1,384,4096]{2,1,0:T(8,128)(2,1)} %param.21) | copy-start | bytes 9437188
  6.5 68.5 %all-gather.5.cloned.1.call-start = ((), (), s32[]{:S(2)}) async-start(), calls=%async_computation.4 | async-start | bytes 4456448 | tf_op jit(solution)/shard_map/all_gather | solution.py:88
  7.3 109.1 %all-gather.3.cloned.1.call-start = ((), (), s32[]{:S(2)}) async-start(), calls=%async_computation.3 | async-start | bytes 2228224 | tf_op jit(solution)/shard_map/all_gather | solution.py:107
  8.0 224.1 %all-reduce.2.cloned.1.call-start = ((), (), s32[]{:S(2)}) async-start(), calls=%async_computation.5 | async-start | bytes 4194304 | tf_op jit(solution)/shard_map/psum | solution.py:106
  79.8 156.8 %copy-start.3 = (f32[4096]{0:T(1024)S(1)}, f32[4096]{0:T(1024)}, u32[]{:S(2)}) copy-start(f32[4096]{0:T(1024)} %param.16) | copy-start | bytes 49156
  235.2 1.4 copy-start.1
  256.3 79.0 %copy-start.5 = (bf16[1,4096,384]{2,1,0:T(8,128)(2,1)S(1)}, bf16[1,4096,384]{2,1,0:T(8,128)(2,1)}, u32[]{:S(2)}) copy-start(bf16[1,4096,384]{2,1,0:T(8,128)(2,1)} %param.19) | copy-start | bytes 9437188
  335.3 3.4 copy-start.6
  347.6 6.0 %copy-start.4 = (bf16[256,8]{0,1:T(8,128)(2,1)S(1)}, bf16[256,8]{0,1:T(8,128)(2,1)}, u32[]{:S(2)}) copy-start(bf16[256,8]{0,1:T(8,128)(2,1)} %param.18) | copy-start | bytes 12292
  347.6 6.0 %copy-start.2 = (s32[256,8]{0,1:T(8,128)S(1)}, s32[256,8]{0,1:T(8,128)}, u32[]{:S(2)}) copy-start(s32[256,8]{0,1:T(8,128)} %param.17) | copy-start | bytes 24580
  347.6 93.4 %all-to-all-start.1 = ((bf16[16,48,4096]{2,1,0:T(8,128)(2,1)}), bf16[16,48,4096]{2,1,0:T(8,128)(2,1)}, u32[]{:S(2)}, u32[]{:S(2)}) async-start(bf16[16,48,4096]{2,1,0:T(8,128)(2,1)} %bitcast.108), calls=%async_computation.1 | async-start | bytes 12582912 | tf_op jit(solution)/shard_map/all_to_all | solution.py:125
  353.6 158.4 %reduce-scatter.2.cloned.1.call-start = ((), (), s32[]{:S(2)}) async-start(), calls=%async_computation.6 | async-start | bytes 2228224 | tf_op jit(solution)/shard_map/reduce_scatter | solution.py:130
Sparse Core Ops, SparseCore 0:
  9.8 65.2 all-gather.4
  76.8 39.4 all-gather.2
  118.7 113.3 all-reduce.1
  447.2 64.7 reduce-scatter.1
where the time goes:
time: 521 us; the launch traced here: 520 us
  waiting for transfers between devices  356 us (68%)
  blocking collectives  79 us (15%)
  matrix products  30.6 us (6%)
  local copies, waits for them, and re-layouts  20.5 us (4%)
  other arithmetic  14.3 us (3%)
  between operations  14 us (3%)
  starting transfers between devices  6.07 us (1%)
    psum x1, waiting for transfers between devices, shards(): lax.psum(head_part.astype(jnp.bfloat16), 'tensor').astype(jnp.float32)  116 us
    all_to_all x1, waiting for transfers between devices, shards(): lax.all_to_all(computed, 'expert', split_axis=0, concat_axis=0, tiled=True)  87.2 us
    all_to_all x1, blocking collectives, shards(): lax.all_to_all(outgoing, 'expert', split_axis=0, concat_axis=0, tiled=True)  79 us
    reduce_scatter x1, waiting for transfers between devices, shards(): lax.psum_scatter(expert_part.astype(jnp.bfloat16), 'tensor', scatter_dime...  65 us
    all_gather x1, waiting for transfers between devices, shards(): lax.all_gather(out_proj, 'expert', axis=1, tiled=True)  51.8 us
    all_gather x1, waiting for transfers between devices, shards(): residual_full = lax.all_gather(residual, 'tensor', axis=0, tiled=True)  34.7 us
    gather x1, local copies, waits for them, and re-layouts, shards(): jnp.take(normed_full, source_rows, axis=0)  13.8 us
  transfers between devices with their start and end apart: 5, of which 5 were waited for; matrix products, arithmetic and copies ran while one was open for 4% of the time, Pallas kernels for 0%

commit v1 on v0

v1 whole, which is shorter than its diff:
```python
import math

import jax
import jax.numpy as jnp
from jax import lax
from jax.sharding import PartitionSpec as P

HEADS = 64
KVH = 4
HD = 128
TOPK = 8
HSPLIT = 4
TOK_DEV = 16
PREFIX = 1024
MOST = 3

F32 = jnp.float32
BF16 = jnp.bfloat16


def chip_swap(array, tensor_count):
    return lax.ppermute(array, "tensor", [(t, t ^ 1) for t in range(tensor_count)])


def along_z(array, groups):
    return lax.all_to_all(
        array, "tensor", split_axis=0, concat_axis=0, tiled=True, axis_index_groups=groups
    )


def attend(queries, keys_values, prefix_len, kv_index):
    step_rows = queries.shape[0]
    per_device = queries.shape[1] // HD
    cached = lax.dynamic_index_in_dim(keys_values[0], kv_index, 0, keepdims=False)
    key_rows = cached[:, :HD]
    value_rows = cached[:, HD:]
    context = cached.shape[0]
    query_rows = queries.reshape(step_rows, per_device, HD)
    scores = jnp.einsum("nhd,cd->hnc", query_rows, key_rows, preferred_element_type=F32) / math.sqrt(HD)
    columns = jnp.arange(context, dtype=jnp.int32)[None, :]
    positions = jnp.arange(step_rows, dtype=jnp.int32)[:, None]
    visible = ((columns < prefix_len[0]) | (columns >= PREFIX) & (columns - PREFIX <= positions))[None]
    highest = jnp.max(jnp.where(visible, scores, -1e30), axis=-1, keepdims=True)
    weights = jnp.exp(jnp.where(visible, scores - highest, -1e30))
    summed = jnp.sum(weights, axis=-1)
    blended = jnp.einsum("hnc,cd->nhd", weights.astype(BF16), value_rows, preferred_element_type=F32)
    attended = (blended / jnp.transpose(summed)[:, :, None]).astype(BF16)
    return attended.reshape(step_rows, per_device * HD)


def shards(
    queries,
    keys_values,
    prefix_len,
    out_proj,
    residual,
    norm_gain,
    expert_ids,
    route_weights,
    w_gate,
    w_up,
    w_down,
):
    tensor_count = lax.axis_size("tensor")
    expert_count = lax.axis_size("expert")
    tensor_index = lax.axis_index("tensor")
    chips = tensor_count // 2
    core = tensor_index % 2
    same_core = [[2 * z + c for z in range(chips)] for c in range(2)]
    per_device = queries.shape[1] // HD
    width = residual.shape[1]
    half_rows = chips * TOK_DEV

    gate_other = chip_swap(w_gate[0], tensor_count)
    up_other = chip_swap(w_up[0], tensor_count)
    down_other = chip_swap(w_down[0], tensor_count)

    slot_index = tensor_index // HSPLIT
    slot_count = tensor_count // HSPLIT
    capacity = chips * MOST
    ids = expert_ids.reshape(chips, 2, TOK_DEV, TOPK)
    ids = lax.dynamic_index_in_dim(ids, core, 1, keepdims=False)
    gains = route_weights.reshape(chips, 2, TOK_DEV, TOPK)
    gains = lax.dynamic_index_in_dim(gains, core, 1, keepdims=False)
    wanted = jnp.arange(expert_count, dtype=jnp.int32) * slot_count + slot_index
    named = ids[:, :, :, None] == wanted
    hits = jnp.sum(named.astype(jnp.int32), axis=2)
    weight = jnp.sum(jnp.where(named, gains[:, :, :, None].astype(F32), 0.0), axis=2)
    earlier = (jnp.arange(TOK_DEV)[:, None] > jnp.arange(TOK_DEV)[None, :]).astype(BF16)
    rank = jnp.einsum("nm,zmj->znj", earlier, hits.astype(BF16), preferred_element_type=F32)
    position = jnp.arange(chips, dtype=jnp.int32)[:, None, None] * MOST + rank.astype(jnp.int32)
    position = jnp.where(hits > 0, position, -1).reshape(half_rows, expert_count)
    weight = weight.reshape(half_rows, expert_count)
    slots = jnp.arange(capacity, dtype=jnp.int32)
    pick = (position.T[:, None, :] == slots[None, :, None]).astype(BF16)
    pick = pick.reshape(expert_count * capacity, half_rows)
    combine = jnp.where(position[:, :, None] == slots[None, None, :], weight[:, :, None], 0.0)
    combine = combine.astype(BF16).reshape(half_rows, expert_count * capacity)

    attended = attend(queries, keys_values, prefix_len, tensor_index * per_device // (HEADS // KVH))
    projection = lax.all_gather(out_proj, "expert", axis=1, tiled=True)
    attended = attended.reshape(chips, 2, TOK_DEV, per_device * HD)
    attended_away = lax.dynamic_index_in_dim(attended, 1 - core, 1, keepdims=False)
    attended_here = lax.dynamic_index_in_dim(attended, core, 1, keepdims=False)
    part_away = jnp.dot(attended_away.reshape(half_rows, -1), projection, preferred_element_type=F32).astype(BF16)
    part_away = chip_swap(part_away, tensor_count)
    part_here = jnp.dot(attended_here.reshape(half_rows, -1), projection, preferred_element_type=F32).astype(BF16)
    chip_part = (part_here.astype(F32) + part_away.astype(F32)).astype(BF16)
    head_parts = along_z(chip_part.reshape(chips, TOK_DEV, width), same_core)
    head_sum = jnp.sum(head_parts.astype(F32), axis=0)
    hidden_state = (residual.astype(F32) + head_sum).astype(BF16)

    values = hidden_state.astype(F32)
    factor = lax.rsqrt(jnp.mean(values * values, axis=-1, keepdims=True) + 1e-06)
    normed = (values * factor * norm_gain[None, :]).astype(BF16)
    normed_half = along_z(jnp.broadcast_to(normed[None], (chips,) + normed.shape), same_core)

    outgoing = jnp.dot(pick, normed_half.reshape(half_rows, width), preferred_element_type=F32).astype(BF16)
    arrived = lax.all_to_all(
        outgoing.reshape(expert_count, capacity, width), "expert", split_axis=0, concat_axis=0, tiled=True
    )
    rows = arrived.reshape(expert_count * capacity, width)

    def inner_of(gate, up):
        gate_val = jnp.dot(rows, gate, preferred_element_type=F32)
        up_val = jnp.dot(rows, up, preferred_element_type=F32)
        return (jax.nn.silu(gate_val) * up_val).astype(BF16)

    result = jnp.dot(inner_of(w_gate[0], w_up[0]), w_down[0], preferred_element_type=F32)
    result = result + jnp.dot(inner_of(gate_other, up_other), down_other, preferred_element_type=F32)
    result = result.astype(BF16).reshape(expert_count, capacity, width)
    returned = lax.all_to_all(result, "expert", split_axis=0, concat_axis=0, tiled=True)
    expert_part = jnp.dot(combine, returned.reshape(expert_count * capacity, width), preferred_element_type=F32)
    expert_parts = along_z(expert_part.astype(BF16).reshape(chips, TOK_DEV, width), same_core)
    expert_sum = jnp.sum(expert_parts.astype(F32), axis=0)
    return (hidden_state.astype(F32) + expert_sum).astype(BF16)


def solution(mesh):
    return jax.shard_map(
        shards,
        mesh=mesh,
        in_specs=(
            P("expert", "tensor"),
            P("expert", None, None, None),
            P("expert"),
            P("tensor", "expert"),
            P(("expert", "tensor"), None),
            P(),
            P("expert", None),
            P("expert", None),
            P(("expert", "tensor"), None, None),
            P(("expert", "tensor"), None, None),
            P(("expert", "tensor"), None, None),
        ),
        out_specs=P(("expert", "tensor"), None),
        check_vma=False,
    )
```

time: 521 us -> 328 us (0.63)
  waiting for transfers between devices: 356 us -> 170 us
  local copies, waits for them, and re-layouts: 20.5 us -> 2.39 us
  matrix products: 30.6 us -> 48.6 us
  starting transfers between devices: 6.07 us -> 19.4 us
  blocking collectives: 79 us -> 66.9 us
  other arithmetic: 14.3 us -> 3.96 us
    psum x1 -> x0, waiting for transfers between devices: 116 us -> none  [shards(): lax.psum(head_part.astype(jnp.bfloat16), 'tensor').astype(jnp.float32)]
    reduce_scatter x1 -> x0, waiting for transfers between devices: 65 us -> none  [shards(): lax.psum_scatter(expert_part.astype(jnp.bfloat16), 'tensor', scatter_dime...]
    all_gather x2 -> x1, waiting for transfers between devices: 86.5 us -> 56.9 us  [shards(): projection = lax.all_gather(out_proj, 'expert', axis=1, tiled=True)]
    all_to_all x1 -> x3, waiting for transfers between devices: 87.2 us -> 109 us  [the longest x1 43.4 us: shards(): lax.all_to_all(outgoing.reshape(expert_count, capacity, width), 'expert',...]
    dot_general x6 -> x10, matrix products: 25.5 us -> 43.5 us  [the longest x1 10.7 us: shards(): jnp.dot(inner_of(gate_other, up_other), down_other, preferred_element_typ...]
    gather x1 -> x0, local copies, waits for them, and re-layouts: 13.8 us -> none  [shards(): jnp.take(normed_full, source_rows, axis=0)]
    all_to_all x1 -> x3, starting transfers between devices: 5.95 us -> 18.7 us  [the longest x1 8.77 us: shards(): lax.all_to_all(result, 'expert', split_axis=0, concat_axis=0, tiled=True)]
    all_to_all x1 -> x2, blocking collectives: 79 us -> 66.9 us  [along_z(): lax.all_to_all(array, 'tensor', split_axis=0, concat_axis=0, tiled=True,...]
  transfers between devices with their start and end apart: 5 -> 8, of which waited for: 5 -> 5; matrix products, arithmetic and copies ran while one was open for 4% -> 10% of each run, Pallas kernels for 0% -> 0%
where the time goes in v1:
time: 328 us; the launch traced here: 325 us
  waiting for transfers between devices  170 us (52%)
  blocking collectives  66.9 us (20%)
  matrix products  48.6 us (15%)
  starting transfers between devices  19.4 us (6%)
  between operations  14.4 us (4%)
  other arithmetic  3.96 us (1%)
    all_to_all x2, blocking collectives, along_z(): lax.all_to_all(array, 'tensor', split_axis=0, concat_axis=0, tiled=True,...  66.9 us
    all_gather x1, waiting for transfers between devices, shards(): projection = lax.all_gather(out_proj, 'expert', axis=1, tiled=True)  56.9 us
    all_to_all x1, waiting for transfers between devices, shards(): lax.all_to_all(outgoing.reshape(expert_count, capacity, width), 'expert',...  43.4 us
    all_to_all x1, waiting for transfers between devices, shards(): lax.all_to_all(result, 'expert', split_axis=0, concat_axis=0, tiled=True)  38.9 us
    all_to_all x1, waiting for transfers between devices, along_z(): lax.all_to_all(array, 'tensor', split_axis=0, concat_axis=0, tiled=True,...  27 us
    dot_general x1, matrix products, shards(): jnp.dot(inner_of(gate_other, up_other), down_other, preferred_element_typ...  10.7 us
    dot_general x2, matrix products, inner_of(): gate_val = jnp.dot(rows, gate, preferred_element_type=F32)  10.1 us
    dot_general x1, matrix products, shards(): jnp.dot(inner_of(w_gate[0], w_up[0]), w_down[0], preferred_element_type=F32)  10 us
  transfers between devices with their start and end apart: 8, of which 5 were waited for; matrix products, arithmetic and copies ran while one was open for 10% of the time, Pallas kernels for 0%

profile of v1, /device:TPU:2, one launch (start us, length us, event | category | flops | bytes accessed | tf_op | source)
XLA Modules:
  0.0 325.1 jit_solution(82748444382406741)
XLA Ops:
  6.5 0.7 all-gather.2.cloned.1.call-update
  8.3 2.0 fusion.13
  10.4 5.1 %fusion.70 = (f32[4,256]{1,0:T(4,128)S(1)}, bf16[4,256,1280]{1,2,0:T(8,128)(2,1)}) fusion(pred[256,1280]{0,1:T(8,128)(4,1)} %fusion.13, bf16[1280,256]{1,0:T(8,128)(2,1)S(1)} %dynamic-slice_bitcast_fusion, bf16[256,512]{1,0:T(8,128)(2,1)} %param.11), kind=kOutput, calls=%fused_computation.92 | convolution fusion | flops 680264960 | bytes 4460544 | tf_op jit(solution)/shard_map/sub | solution.py:44
  15.5 2.3 fusion.21
  18.1 56.9 %all-gather.2.cloned.1.call-done = bf16[512,4096]{1,0:T(8,128)(2,1)} async-done(((bf16[512,256]{1,0:T(8,128)(2,1)}), bf16[512,4096]{1,0:T(8,128)(2,1)}) %all-gather.2.cloned.1.call-update) | async-done | bytes 4194320 | tf_op jit(solution)/shard_map/all_gather | solution.py:101
  75.0 3.1 convolution_convert_fusion.1
  78.2 2.6 collective-permute-done
  80.8 0.7 add_convert_fusion.1
  81.6 36.0 %all_to_all.25 = bf16[8,16,4096]{2,1,0:T(8,128)(2,1)S(1)} all-to-all(bf16[8,16,4096]{2,1,0:T(8,128)(2,1)S(1)} %bitcast.116), channel_id=1, replica_groups={{0,2,4,6,8,10,12,14},{1,3,5,7,9,11,13,15},{16,18,20,22,24,26,28,30},{17..., dimensions={0} | all-to-all | bytes 2097152 | tf_op jit(solution)/shard_map/all_to_all | solution.py:26
  118.0 1.1 broadcast_in_dim.76
  119.1 4.2 %all-to-all-start.1 = ((bf16[8,16,4096]{2,1,0:T(8,128)(2,1)}), bf16[8,16,4096]{2,1,0:T(8,128)(2,1)}, u32[]{:S(2)}, u32[]{:S(2)}) async-start(bf16[8,16,4096]{2,1,0:T(8,128)(2,1)} %broadcast_in_dim.76), calls=%async_computation.1 | async-start | bytes 2097152 | tf_op jit(solution)/shard_map/all_to_all | solution.py:26
  124.3 27.0 %all-to-all-done.1 = bf16[8,16,4096]{2,1,0:T(8,128)(2,1)} async-done(((bf16[8,16,4096]{2,1,0:T(8,128)(2,1)}), bf16[8,16,4096]{2,1,0:T(8,128)(2,1)}, u32[]{:S(2)}, u32[]{:S(2)}) %all-to-all-start.1) | async-done | bytes 1048608 | tf_op jit(solution)/shard_map/all_to_all | solution.py:26
  151.2 3.8 %convolution_convert_fusion = bf16[384,4096]{1,0:T(8,128)(2,1)} fusion(pred[384,128]{1,0:T(8,128)(4,1)S(1)} %bitcast.122, bf16[128,4096]{1,0:T(8,128)(2,1)} %bitcast.17), kind=kOutput, calls=%fused_computation.2 | convolution fusion | flops 404226048 | bytes 4243456 | tf_op jit(solution)/shard_map/dot_general | solution.py:118
  155.1 5.7 %all-to-all-start.2 = ((bf16[16,24,4096]{2,1,0:T(8,128)(2,1)}), bf16[16,24,4096]{2,1,0:T(8,128)(2,1)}, u32[]{:S(2)}, u32[]{:S(2)}) async-start(bf16[16,24,4096]{2,1,0:T(8,128)(2,1)} %bitcast.114), calls=%async_computation.2 | async-start | bytes 6291456 | tf_op jit(solution)/shard_map/all_to_all | solution.py:119
  161.4 43.4 %all-to-all-done.2 = bf16[16,24,4096]{2,1,0:T(8,128)(2,1)} async-done(((bf16[16,24,4096]{2,1,0:T(8,128)(2,1)}), bf16[16,24,4096]{2,1,0:T(8,128)(2,1)}, u32[]{:S(2)}, u32[]{:S(2)}) %all-to-all-start.2) | async-done | bytes 3145760 | tf_op jit(solution)/shard_map/all_to_all | solution.py:119
  204.8 5.4 %fusion.63 = f32[384,384]{1,0:T(8,128)} fusion(bf16[384,4096]{1,0:T(8,128)(2,1)} %bitcast.19, bf16[1,4096,384]{2,1,0:T(8,128)(2,1)} %param.19), kind=kOutput, calls=%fused_computation.85 | convolution fusion | flops 1207959552 | bytes 6881280 | tf_op jit(solution)/shard_map/dot_general | solution.py:125
  210.2 4.6 %fusion.77 = f32[384,384]{1,0:T(8,128)S(1)} fusion(bf16[384,4096]{1,0:T(8,128)(2,1)} %bitcast.19, bf16[4096,384]{1,0:T(8,128)(2,1)} %collective-permute-done.1), kind=kOutput, calls=%fused_computation.94 | convolution fusion | flops 1207959552 | bytes 6881280 | tf_op jit(solution)/shard_map/dot_general | solution.py:125
  214.9 10.0 %fusion.24 = f32[384,4096]{1,0:T(8,128)} fusion(bf16[384,4096]{1,0:T(8,128)(2,1)} %bitcast.19, f32[384,384]{1,0:T(8,128)} %fusion.63, bf16[1,384,4096]{2,1,0:T(8,128)(2,1)} %param.21, bf16[1,4096,384]{2,1,0:T(8,128)(2,1)} %param.20), kind=kOutput, calls=%fused_computation.30 | convolution fusion | flops 2416803840 | bytes 16318464 | tf_op jit(solution)/shard_map/dot_general | solution.py:129
  224.9 10.7 %add_convert_fusion = bf16[384,4096]{1,0:T(8,128)(2,1)} fusion(f32[384,4096]{1,0:T(8,128)} %fusion.24, bf16[384,4096]{1,0:T(8,128)(2,1)} %collective-permute-done.3, f32[384,384]{1,0:T(8,128)S(1)} %fusion.77, bf16[384,4096]{1,0:T(8,128)(2,1)} %bitcast.19, bf16[4096,384]{1,0:T(8,128)(2,1)} %collective-permute-done.2), kind=kOutput, calls=%fused_computation.1 | convolution fusion | flops 2419949568 | bytes 19464192 | tf_op jit(solution)/shard_map/dot_general | solution.py:130
  235.6 8.8 %all-to-all-start.3 = ((bf16[16,24,4096]{2,1,0:T(8,128)(2,1)}), bf16[16,24,4096]{2,1,0:T(8,128)(2,1)}, u32[]{:S(2)}, u32[]{:S(2)}) async-start(bf16[16,24,4096]{2,1,0:T(8,128)(2,1)} %bitcast.115), calls=%async_computation.3 | async-start | bytes 6291456 | tf_op jit(solution)/shard_map/all_to_all | solution.py:132
  245.0 38.9 %all-to-all-done.3 = bf16[16,24,4096]{2,1,0:T(8,128)(2,1)} async-done(((bf16[16,24,4096]{2,1,0:T(8,128)(2,1)}), bf16[16,24,4096]{2,1,0:T(8,128)(2,1)}, u32[]{:S(2)}, u32[]{:S(2)}) %all-to-all-start.3) | async-done | bytes 3145760 | tf_op jit(solution)/shard_map/all_to_all | solution.py:132
  283.9 2.6 fusion.5
  286.5 30.9 %all_to_all.26 = bf16[8,16,4096]{2,1,0:T(8,128)(2,1)S(1)} all-to-all(bf16[8,16,4096]{2,1,0:T(8,128)(2,1)S(1)} %bitcast.117), channel_id=1, replica_groups={{0,2,4,6,8,10,12,14},{1,3,5,7,9,11,13,15},{16,18,20,22,24,26,28,30},{17..., dimensions={0} | all-to-all | bytes 2097152 | tf_op jit(solution)/shard_map/all_to_all | solution.py:26
  317.6 0.7 fusion.42
  (47 shorter events, 3.4 us)
Async XLA Ops:
  6.5 1.7 copy-start
  6.5 68.5 %all-gather.2.cloned.1.call-start = ((), (), s32[]{:S(2)}) async-start(), calls=%async_computation.5 | async-start | bytes 4456448 | tf_op jit(solution)/shard_map/all_gather | solution.py:101
  75.0 5.8 %copy-start.1 = (bf16[512,4096]{1,0:T(8,128)(2,1)S(1)}, bf16[512,4096]{1,0:T(8,128)(2,1)}, u32[]{:S(2)}) copy-start(bf16[512,4096]{1,0:T(8,128)(2,1)} %all-gather.2.cloned.1.call-done) | copy-start | bytes 12582916
  78.1 2.7 collective-permute-start
  81.6 36.1 %copy-start.2 = (bf16[16,4096]{1,0:T(8,128)(2,1)S(1)}, bf16[16,4096]{1,0:T(8,128)(2,1)}, u32[]{:S(2)}) copy-start(bf16[16,4096]{1,0:T(8,128)(2,1)} %param.15) | copy-start | bytes 393220
  81.6 36.3 %copy-start.3 = (f32[4096]{0:T(1024)S(1)}, f32[4096]{0:T(1024)}, u32[]{:S(2)}) copy-start(f32[4096]{0:T(1024)} %param.16) | copy-start | bytes 49156
  117.6 5.8 %copy-start.4 = (s32[256,8]{0,1:T(8,128)S(1)}, s32[256,8]{0,1:T(8,128)}, u32[]{:S(2)}) copy-start(s32[256,8]{0,1:T(8,128)} %param.17) | copy-start | bytes 24580
  119.1 32.2 %all-to-all-start.1 = ((bf16[8,16,4096]{2,1,0:T(8,128)(2,1)}), bf16[8,16,4096]{2,1,0:T(8,128)(2,1)}, u32[]{:S(2)}, u32[]{:S(2)}) async-start(bf16[8,16,4096]{2,1,0:T(8,128)(2,1)} %broadcast_in_dim.76), calls=%async_computation.1 | async-start | bytes 2097152 | tf_op jit(solution)/shard_map/all_to_all | solution.py:26
  155.1 49.7 %all-to-all-start.2 = ((bf16[16,24,4096]{2,1,0:T(8,128)(2,1)}), bf16[16,24,4096]{2,1,0:T(8,128)(2,1)}, u32[]{:S(2)}, u32[]{:S(2)}) async-start(bf16[16,24,4096]{2,1,0:T(8,128)(2,1)} %bitcast.114), calls=%async_computation.2 | async-start | bytes 6291456 | tf_op jit(solution)/shard_map/all_to_all | solution.py:119
  160.8 49.4 %collective-permute-start.1 = (bf16[4096,384]{1,0:T(8,128)(2,1)}, bf16[4096,384]{1,0:T(8,128)(2,1)}, u32[]{:S(2)}, u32[]{:S(2)}) collective-permute-start(bf16[4096,384]{1,0:T(8,128)(2,1)} %bitcast.127), channel_id=1, source_target_pairs={{0,1},{1,0},{2,3},{3,2},{4,5},{5,4},{6,7},{7,6},{8,9},{9,8},{10,11... | collective-permute-start | bytes 9437192 | tf_op jit(solution)/shard_map/ppermute | solution.py:22
  160.8 64.1 %collective-permute-start.3 = (bf16[384,4096]{1,0:T(8,128)(2,1)}, bf16[384,4096]{1,0:T(8,128)(2,1)}, u32[]{:S(2)}, u32[]{:S(2)}) collective-permute-start(bf16[384,4096]{1,0:T(8,128)(2,1)} %bitcast.118), channel_id=1, source_target_pairs={{0,1},{1,0},{2,3},{3,2},{4,5},{5,4},{6,7},{7,6},{8,9},{9,8},{10,11... | collective-permute-start | bytes 9437192 | tf_op jit(solution)/shard_map/ppermute | solution.py:22
  161.3 63.6 %collective-permute-start.2 = (bf16[4096,384]{1,0:T(8,128)(2,1)}, bf16[4096,384]{1,0:T(8,128)(2,1)}, u32[]{:S(2)}, u32[]{:S(2)}) collective-permute-start(bf16[4096,384]{1,0:T(8,128)(2,1)} %bitcast.119), channel_id=1, source_target_pairs={{0,1},{1,0},{2,3},{3,2},{4,5},{5,4},{6,7},{7,6},{8,9},{9,8},{10,11... | collective-permute-start | bytes 9437192 | tf_op jit(solution)/shard_map/ppermute | solution.py:22
  235.6 8.8 %copy-start.5 = (bf16[256,8]{0,1:T(8,128)(2,1)S(1)}, bf16[256,8]{0,1:T(8,128)(2,1)}, u32[]{:S(2)}) copy-start(bf16[256,8]{0,1:T(8,128)(2,1)} %param.18) | copy-start | bytes 12292
  235.6 48.3 %all-to-all-start.3 = ((bf16[16,24,4096]{2,1,0:T(8,128)(2,1)}), bf16[16,24,4096]{2,1,0:T(8,128)(2,1)}, u32[]{:S(2)}, u32[]{:S(2)}) async-start(bf16[16,24,4096]{2,1,0:T(8,128)(2,1)} %bitcast.115), calls=%async_computation.3 | async-start | bytes 6291456 | tf_op jit(solution)/shard_map/all_to_all | solution.py:132
Sparse Core Ops, SparseCore 0:
  9.8 65.2 all-gather.1

commit v2 on v1

--- a/solution.py
+++ b/solution.py
@@ -20,6 +20,20 @@
 
 def chip_swap(array, tensor_count):
     return lax.ppermute(array, "tensor", [(t, t ^ 1) for t in range(tensor_count)])
+
+
+def shift(array, down, right, rows, columns):
+    pairs = [
+        (y * columns + x, (y + down) % rows * columns + (x + right) % columns)
+        for y in range(rows)
+        for x in range(columns)
+    ]
+    return lax.ppermute(array, "expert", pairs)
+
+
+def ordered(pieces, index):
+    count = len(pieces)
+    return [lax.select_n((index - place) % count, *pieces) for place in range(count)]
 
 
 def along_z(array, groups):
@@ -97,18 +111,36 @@
     combine = jnp.where(position[:, :, None] == slots[None, None, :], weight[:, :, None], 0.0)
     combine = combine.astype(BF16).reshape(half_rows, expert_count * capacity)
 
+    side_y = side_x = math.isqrt(expert_count)
+    expert_index = lax.axis_index("expert")
+    place_y, place_x = expert_index // side_x, expert_index % side_x
+    part_width = out_proj.shape[1]
+    blocks = [out_proj] + [shift(out_proj, d, 0, side_y, side_x) for d in range(1, side_y)]
+    projection = jnp.concatenate(ordered(blocks, place_y), axis=1)
+
     attended = attend(queries, keys_values, prefix_len, tensor_index * per_device // (HEADS // KVH))
-    projection = lax.all_gather(out_proj, "expert", axis=1, tiled=True)
     attended = attended.reshape(chips, 2, TOK_DEV, per_device * HD)
-    attended_away = lax.dynamic_index_in_dim(attended, 1 - core, 1, keepdims=False)
-    attended_here = lax.dynamic_index_in_dim(attended, core, 1, keepdims=False)
-    part_away = jnp.dot(attended_away.reshape(half_rows, -1), projection, preferred_element_type=F32).astype(BF16)
+    attended = [lax.dynamic_index_in_dim(attended, c, 1, keepdims=False) for c in (1 - core, core)]
+    attended = jnp.stack(attended).reshape(2, half_rows, per_device * HD)
+    pieces = [attended] + [shift(attended, 0, d, side_y, side_x) for d in range(1, side_x)]
+    rows_away = jnp.concatenate([piece[0] for piece in pieces], axis=0)
+    rows_here = jnp.concatenate([piece[1] for piece in pieces], axis=0)
+    part_away = jnp.dot(rows_away, projection, preferred_element_type=F32).astype(BF16)
     part_away = chip_swap(part_away, tensor_count)
-    part_here = jnp.dot(attended_here.reshape(half_rows, -1), projection, preferred_element_type=F32).astype(BF16)
+    part_here = jnp.dot(rows_here, projection, preferred_element_type=F32).astype(BF16)
     chip_part = (part_here.astype(F32) + part_away.astype(F32)).astype(BF16)
-    head_parts = along_z(chip_part.reshape(chips, TOK_DEV, width), same_core)
-    head_sum = jnp.sum(head_parts.astype(F32), axis=0)
-    hidden_state = (residual.astype(F32) + head_sum).astype(BF16)
+    chip_part = chip_part.reshape(side_x, chips, TOK_DEV, side_y * part_width)
+    chip_part = jnp.transpose(chip_part, (1, 0, 2, 3))
+    chip_part, pick, combine, gate_other, up_other, down_other, residual, norm_gain = lax.optimization_barrier(
+        (chip_part, pick, combine, gate_other, up_other, down_other, residual, norm_gain)
+    )
+    head_parts = along_z(chip_part, same_core)
+    sums = jnp.sum(head_parts.astype(F32), axis=0).astype(BF16)
+    sums = [sums[0]] + [shift(sums[d], 0, -d, side_y, side_x) for d in range(1, side_x)]
+    sums = [one.reshape(TOK_DEV, side_y, part_width) for one in sums]
+    sums = [sums[0]] + sums[:0:-1]
+    head_sum = jnp.stack(ordered(sums, place_x), axis=2).reshape(TOK_DEV, width)
+    hidden_state = (residual.astype(F32) + head_sum.astype(F32)).astype(BF16)
 
     values = hidden_state.astype(F32)
     factor = lax.rsqrt(jnp.mean(values * values, axis=-1, keepdims=True) + 1e-06)

time: 328 us -> 273 us (0.83)
  waiting for transfers between devices: 170 us -> 20.1 us
  blocking collectives: 66.9 us -> 177 us
  between operations: 14.4 us -> 1.12 us
  matrix products: 48.6 us -> 41.1 us
  local copies, waits for them, and re-layouts: 2.39 us -> 7.68 us
  other arithmetic: 3.96 us -> 7.53 us
    all_to_all x3 -> x0, waiting for transfers between devices: 109 us -> none  [the longest x1 43.4 us: shards(): lax.all_to_all(outgoing.reshape(expert_count, capacity, width), 'expert',...]
    all_to_all x0 -> x2, blocking collectives: none -> 81.8 us  [the longest x1 42.4 us: shards(): lax.all_to_all(outgoing.reshape(expert_count, capacity, width), 'expert',...]
    all_gather x1 -> x0, waiting for transfers between devices: 56.9 us -> none  [shards(): projection = lax.all_gather(out_proj, 'expert', axis=1, tiled=True)]
    all_to_all x2 -> x3, blocking collectives: 66.9 us -> 95.6 us  [along_z(): lax.all_to_all(array, 'tensor', split_axis=0, concat_axis=0, tiled=True,...]
    ppermute x0 -> x9, waiting for transfers between devices: none -> 19.1 us  [shift(): return lax.ppermute(array, 'expert', pairs)]
    all_to_all x3 -> x0, starting transfers between devices: 18.7 us -> none  [the longest x1 8.77 us: shards(): lax.all_to_all(result, 'expert', split_axis=0, concat_axis=0, tiled=True)]
    ppermute x0 -> x9, starting transfers between devices: none -> 16.5 us  [shift(): return lax.ppermute(array, 'expert', pairs)]
    squeeze x0 -> x3, local copies, waits for them, and re-layouts: none -> 4.26 us  [shards(): rows_here = jnp.concatenate([piece[1] for piece in pieces], axis=0)]
  transfers between devices with their start and end apart: 8 -> 13, of which waited for: 5 -> 7; matrix products, arithmetic and copies ran while one was open for 10% -> 8% of each run, Pallas kernels for 0% -> 0%
where the time goes in v2:
time: 273 us; the launch traced here: 272 us
  blocking collectives  177 us (65%)
  matrix products  41.1 us (15%)
  waiting for transfers between devices  20.1 us (7%)
  starting transfers between devices  17.2 us (6%)
  local copies, waits for them, and re-layouts  7.68 us (3%)
  other arithmetic  7.53 us (3%)
    all_to_all x3, blocking collectives, along_z(): lax.all_to_all(array, 'tensor', split_axis=0, concat_axis=0, tiled=True,...  95.6 us
    all_to_all x1, blocking collectives, shards(): lax.all_to_all(outgoing.reshape(expert_count, capacity, width), 'expert',...  42.4 us
    all_to_all x1, blocking collectives, shards(): lax.all_to_all(result, 'expert', split_axis=0, concat_axis=0, tiled=True)  39.4 us
    ppermute x9, waiting for transfers between devices, shift(): return lax.ppermute(array, 'expert', pairs)  19.1 us
    ppermute x9, starting transfers between devices, shift(): return lax.ppermute(array, 'expert', pairs)  16.5 us
    dot_general x1, matrix products, shards(): jnp.dot(inner_of(gate_other, up_other), down_other, preferred_element_typ...  10.7 us
    dot_general x1, matrix products, shards(): jnp.dot(inner_of(w_gate[0], w_up[0]), w_down[0], preferred_element_type=F32)  10 us
    dot_general x2, matrix products, inner_of(): gate_val = jnp.dot(rows, gate, preferred_element_type=F32)  6.31 us
  transfers between devices with their start and end apart: 13, of which 7 were waited for; matrix products, arithmetic and copies ran while one was open for 8% of the time, Pallas kernels for 0%

profile of v2, /device:TPU:2, one launch (start us, length us, event | category | flops | bytes accessed | tf_op | source)
XLA Modules:
  0.0 272.2 jit_solution(15323627786235245494)
XLA Ops:
  2.8 2.1 fusion.11
  4.9 5.1 %fusion.83 = (f32[4,256]{1,0:T(4,128)S(1)}, bf16[4,256,1280]{1,2,0:T(8,128)(2,1)}) fusion(pred[256,1280]{0,1:T(8,128)(4,1)} %fusion.11, bf16[1280,256]{1,0:T(8,128)(2,1)S(1)} %dynamic-slice_bitcast_fusion, bf16[256,512]{1,0:T(8,128)(2,1)} %param.11), kind=kOutput, calls=%fused_computation.129 | convolution fusion | flops 680264960 | bytes 4460544 | tf_op jit(solution)/shard_map/sub | solution.py:58
  10.0 3.0 %fusion.19 = bf16[256,4,128]{0,2,1:T(8,128)(2,1)} fusion(bf16[4,256,1280]{1,2,0:T(8,128)(2,1)} %get-tuple-element.48, bf16[1280,256]{1,0:T(8,128)(2,1)S(1)} %dynamic-slice_bitcast_fusion, f32[256,4]{0,1:T(4,128)S(1)} %bitcast.164), kind=kOutput, calls=%fused_computation.26 | convolution fusion | flops 335806464 | bytes 3215360 | tf_op jit(solution)/shard_map/hnc,cd->nhd/dot_general | solution.py:60
  15.6 1.7 collective-permute-start.1
  17.4 5.8 %collective-permute-done.2 = bf16[2,128,512]{2,1,0:T(8,128)(2,1)S(1)} collective-permute-done((bf16[2,128,512]{2,1,0:T(8,128)(2,1)S(1)}, bf16[2,128,512]{2,1,0:T(8,128)(2,1)S(1)}, u32[]{:S(2)}, u32[]{:S(2)}) %collective-permute-start.2) | collective-permute-done | bytes 262176 | tf_op jit(solution)/shard_map/ppermute | solution.py:31
  23.8 1.9 collective-permute-start
  26.7 3.1 %collective-permute-done.1 = bf16[2,128,512]{2,1,0:T(8,128)(2,1)} collective-permute-done((bf16[2,128,512]{2,1,0:T(8,128)(2,1)S(1)}, bf16[2,128,512]{2,1,0:T(8,128)(2,1)}, u32[]{:S(2)}, u32[]{:S(2)}) %collective-permute-start.1) | collective-permute-done | bytes 262176 | tf_op jit(solution)/shard_map/ppermute | solution.py:31
  29.8 2.9 %collective-permute-start.4 = (bf16[512,256]{1,0:T(8,128)(2,1)S(1)}, bf16[512,256]{1,0:T(8,128)(2,1)S(1)}, u32[]{:S(2)}, u32[]{:S(2)}) collective-permute-start(bf16[512,256]{1,0:T(8,128)(2,1)S(1)} %copy-done.2), channel_id=1, source_target_pairs={{0,128},{16,144},{32,160},{48,176},{64,192},{80,208},{96,224},{112... | collective-permute-start | bytes 786440 | tf_op jit(solution)/shard_map/ppermute | solution.py:31
  32.7 3.7 %collective-permute-done = bf16[2,128,512]{2,1,0:T(8,128)(2,1)} collective-permute-done((bf16[2,128,512]{2,1,0:T(8,128)(2,1)S(1)}, bf16[2,128,512]{2,1,0:T(8,128)(2,1)}, u32[]{:S(2)}, u32[]{:S(2)}) %collective-permute-start) | collective-permute-done | bytes 262176 | tf_op jit(solution)/shard_map/ppermute | solution.py:31
  39.7 3.9 %collective-permute-done.5 = bf16[512,256]{1,0:T(8,128)(2,1)S(1)} collective-permute-done((bf16[512,256]{1,0:T(8,128)(2,1)S(1)}, bf16[512,256]{1,0:T(8,128)(2,1)S(1)}, u32[]{:S(2)}, u32[]{:S(2)}) %collective-permute-start.5) | collective-permute-done | bytes 262176 | tf_op jit(solution)/shard_map/ppermute | solution.py:31
  44.7 1.7 convolution_convert_fusion.2
  49.7 2.4 add_convert_fusion.1
  52.2 37.4 %all_to_all.25 = bf16[8,4,16,1024]{3,2,1,0:T(8,128)(2,1)} all-to-all(bf16[8,4,16,1024]{3,2,1,0:T(8,128)(2,1)S(1)} %bitcast.149), channel_id=1, replica_groups={{0,2,4,6,8,10,12,14},{1,3,5,7,9,11,13,15},{16,18,20,22,24,26,28,30},{17..., dimensions={0} | all-to-all | bytes 2097152 | tf_op jit(solution)/shard_map/all_to_all | solution.py:40
  91.1 4.1 %collective-permute-start.12 = (bf16[16,1024]{1,0:T(8,128)(2,1)S(1)}, bf16[16,1024]{1,0:T(8,128)(2,1)S(1)}, u32[]{:S(2)}, u32[]{:S(2)}) collective-permute-start(bf16[16,1024]{1,0:T(8,128)(2,1)S(1)} %get-tuple-element.36), channel_id=1, source_target_pairs={{0,48},{16,0},{32,16},{48,32},{64,112},{80,64},{96,80},{112,96},{1... | collective-permute-start | bytes 98312 | tf_op jit(solution)/shard_map/ppermute | solution.py:31
  95.2 1.7 collective-permute-start.11
  98.2 2.4 collective-permute-done.11
  102.6 28.8 %all_to_all.26 = bf16[8,16,4096]{2,1,0:T(8,128)(2,1)S(1)} all-to-all(bf16[8,16,4096]{2,1,0:T(8,128)(2,1)S(1)} %broadcast_in_dim.79), channel_id=1, replica_groups={{0,2,4,6,8,10,12,14},{1,3,5,7,9,11,13,15},{16,18,20,22,24,26,28,30},{17..., dimensions={0} | all-to-all | bytes 2097152 | tf_op jit(solution)/shard_map/all_to_all | solution.py:40
  132.3 42.4 %all_to_all.27 = bf16[16,24,4096]{2,1,0:T(8,128)(2,1)S(1)} all-to-all(bf16[16,24,4096]{2,1,0:T(8,128)(2,1)S(1)} %bitcast.146), channel_id=1, replica_groups=mesh['expert'=16,'tensor'=16] {'expert'}, dimensions={0} | all-to-all | bytes 6291456 | tf_op jit(solution)/shard_map/all_to_all | solution.py:151
  174.7 2.6 fusion.76
  177.4 3.7 %fusion.90 = f32[384,384]{1,0:T(8,128)S(1)} fusion(bf16[384,4096]{1,0:T(8,128)(2,1)S(1)} %bitcast.143, bf16[4096,384]{1,0:T(8,128)(2,1)} %collective-permute-done.7), kind=kOutput, calls=%fused_computation.131 | convolution fusion | flops 1207959552 | bytes 6881280 | tf_op jit(solution)/shard_map/dot_general | solution.py:157
  181.0 10.0 %fusion.22 = f32[384,4096]{1,0:T(8,128)} fusion(bf16[384,4096]{1,0:T(8,128)(2,1)} %bitcast.144, f32[384,384]{1,0:T(8,128)} %fusion.76, bf16[1,384,4096]{2,1,0:T(8,128)(2,1)} %param.21, bf16[1,4096,384]{2,1,0:T(8,128)(2,1)} %param.20), kind=kOutput, calls=%fused_computation.27 | convolution fusion | flops 2416803840 | bytes 16318464 | tf_op jit(solution)/shard_map/dot_general | solution.py:161
  191.1 10.7 %add_convert_fusion = bf16[384,4096]{1,0:T(8,128)(2,1)} fusion(f32[384,4096]{1,0:T(8,128)} %fusion.22, bf16[384,4096]{1,0:T(8,128)(2,1)} %collective-permute-done.9, f32[384,384]{1,0:T(8,128)S(1)} %fusion.90, bf16[384,4096]{1,0:T(8,128)(2,1)} %bitcast.145, bf16[4096,384]{1,0:T(8,128)(2,1)} %collective-permute-done.8), kind=kOutput, calls=%fused_computation.1 | convolution fusion | flops 2419949568 | bytes 19464192 | tf_op jit(solution)/shard_map/dot_general | solution.py:162
  201.8 39.4 %all_to_all.28 = bf16[16,24,4096]{2,1,0:T(8,128)(2,1)S(1)} all-to-all(bf16[16,24,4096]{2,1,0:T(8,128)(2,1)} %bitcast.147), channel_id=1, replica_groups=mesh['expert'=16,'tensor'=16] {'expert'}, dimensions={0} | all-to-all | bytes 6291456 | tf_op jit(solution)/shard_map/all_to_all | solution.py:164
  241.9 29.5 %all_to_all.29 = bf16[8,16,4096]{2,1,0:T(8,128)(2,1)S(1)} all-to-all(bf16[8,16,4096]{2,1,0:T(8,128)(2,1)S(1)} %bitcast.151), channel_id=1, replica_groups={{0,2,4,6,8,10,12,14},{1,3,5,7,9,11,13,15},{16,18,20,22,24,26,28,30},{17..., dimensions={0} | all-to-all | bytes 2097152 | tf_op jit(solution)/shard_map/all_to_all | solution.py:40
  (92 shorter events, 21.2 us)
Async XLA Ops:
  0.0 2.8 %copy-start = (bf16[1,4,1280,256]{3,2,1,0:T(8,128)(2,1)S(1)}, bf16[1,4,1280,256]{3,2,1,0:T(8,128)(2,1)}, u32[]{:S(2)}) copy-start(bf16[1,4,1280,256]{3,2,1,0:T(8,128)(2,1)} %param.12) | copy-start | bytes 7864324
  0.0 15.6 %collective-permute-start.3 = (bf16[512,256]{1,0:T(8,128)(2,1)}, bf16[512,256]{1,0:T(8,128)(2,1)}, u32[]{:S(2)}, u32[]{:S(2)}) collective-permute-start(bf16[512,256]{1,0:T(8,128)(2,1)} %param.14), channel_id=1, source_target_pairs={{0,64},{16,80},{32,96},{48,112},{64,128},{80,144},{96,160},{112,17... | collective-permute-start | bytes 786440 | tf_op jit(solution)/shard_map/ppermute | solution.py:31
  1.6 50.6 %collective-permute-start.9 = (bf16[384,4096]{1,0:T(8,128)(2,1)}, bf16[384,4096]{1,0:T(8,128)(2,1)}, u32[]{:S(2)}, u32[]{:S(2)}) collective-permute-start(bf16[384,4096]{1,0:T(8,128)(2,1)} %bitcast.152), channel_id=1, source_target_pairs={{0,1},{1,0},{2,3},{3,2},{4,5},{5,4},{6,7},{7,6},{8,9},{9,8},{10,11... | collective-permute-start | bytes 9437192 | tf_op jit(solution)/shard_map/ppermute | solution.py:22
  1.6 50.6 %collective-permute-start.8 = (bf16[4096,384]{1,0:T(8,128)(2,1)}, bf16[4096,384]{1,0:T(8,128)(2,1)}, u32[]{:S(2)}, u32[]{:S(2)}) collective-permute-start(bf16[4096,384]{1,0:T(8,128)(2,1)} %bitcast.153), channel_id=1, source_target_pairs={{0,1},{1,0},{2,3},{3,2},{4,5},{5,4},{6,7},{7,6},{8,9},{9,8},{10,11... | collective-permute-start | bytes 9437192 | tf_op jit(solution)/shard_map/ppermute | solution.py:22
  2.1 50.1 %collective-permute-start.7 = (bf16[4096,384]{1,0:T(8,128)(2,1)}, bf16[4096,384]{1,0:T(8,128)(2,1)}, u32[]{:S(2)}, u32[]{:S(2)}) collective-permute-start(bf16[4096,384]{1,0:T(8,128)(2,1)} %bitcast.163), channel_id=1, source_target_pairs={{0,1},{1,0},{2,3},{3,2},{4,5},{5,4},{6,7},{7,6},{8,9},{9,8},{10,11... | collective-permute-start | bytes 9437192 | tf_op jit(solution)/shard_map/ppermute | solution.py:22
  10.0 19.8 %copy-start.2 = (bf16[512,256]{1,0:T(8,128)(2,1)S(1)}, bf16[512,256]{1,0:T(8,128)(2,1)}, u32[]{:S(2)}) copy-start(bf16[512,256]{1,0:T(8,128)(2,1)} %param.14) | copy-start | bytes 786436
  14.3 8.8 %collective-permute-start.2 = (bf16[2,128,512]{2,1,0:T(8,128)(2,1)S(1)}, bf16[2,128,512]{2,1,0:T(8,128)(2,1)S(1)}, u32[]{:S(2)}, u32[]{:S(2)}) collective-permute-start(bf16[2,128,512]{2,1,0:T(8,128)(2,1)S(1)} %pad_maximum_fusion.1), channel_id=1, source_target_pairs={{0,48},{16,0},{32,16},{48,32},{64,112},{80,64},{96,80},{112,96},{1... | collective-permute-start | bytes 786440 | tf_op jit(solution)/shard_map/ppermute | solution.py:31
  15.6 14.1 %collective-permute-start.1 = (bf16[2,128,512]{2,1,0:T(8,128)(2,1)S(1)}, bf16[2,128,512]{2,1,0:T(8,128)(2,1)}, u32[]{:S(2)}, u32[]{:S(2)}) collective-permute-start(bf16[2,128,512]{2,1,0:T(8,128)(2,1)S(1)} %pad_maximum_fusion.1), channel_id=1, source_target_pairs={{0,32},{16,48},{32,0},{48,16},{64,96},{80,112},{96,64},{112,80},{1... | collective-permute-start | bytes 786440 | tf_op jit(solution)/shard_map/ppermute | solution.py:31
  23.8 12.6 %collective-permute-start = (bf16[2,128,512]{2,1,0:T(8,128)(2,1)S(1)}, bf16[2,128,512]{2,1,0:T(8,128)(2,1)}, u32[]{:S(2)}, u32[]{:S(2)}) collective-permute-start(bf16[2,128,512]{2,1,0:T(8,128)(2,1)S(1)} %pad_maximum_fusion.1), channel_id=1, source_target_pairs={{0,16},{16,32},{32,48},{48,0},{64,80},{80,96},{96,112},{112,64},{1... | collective-permute-start | bytes 786440 | tf_op jit(solution)/shard_map/ppermute | solution.py:31
  29.8 9.9 %collective-permute-start.4 = (bf16[512,256]{1,0:T(8,128)(2,1)S(1)}, bf16[512,256]{1,0:T(8,128)(2,1)S(1)}, u32[]{:S(2)}, u32[]{:S(2)}) collective-permute-start(bf16[512,256]{1,0:T(8,128)(2,1)S(1)} %copy-done.2), channel_id=1, source_target_pairs={{0,128},{16,144},{32,160},{48,176},{64,192},{80,208},{96,224},{112... | collective-permute-start | bytes 786440 | tf_op jit(solution)/shard_map/ppermute | solution.py:31
  36.4 7.2 %collective-permute-start.5 = (bf16[512,256]{1,0:T(8,128)(2,1)S(1)}, bf16[512,256]{1,0:T(8,128)(2,1)S(1)}, u32[]{:S(2)}, u32[]{:S(2)}) collective-permute-start(bf16[512,256]{1,0:T(8,128)(2,1)S(1)} %copy-done.2), channel_id=1, source_target_pairs={{0,192},{16,208},{32,224},{48,240},{64,0},{80,16},{96,32},{112,48}... | collective-permute-start | bytes 786440 | tf_op jit(solution)/shard_map/ppermute | solution.py:31
  44.7 1.8 copy-start.3
  44.7 1.7 copy-start.4
  44.7 1.7 copy-start.5
  44.7 1.7 copy-start.6
  44.7 2.1 copy-start.10
  44.7 2.3 copy-start.9
  46.4 3.3 %collective-permute-start.6 = (bf16[512,1024]{1,0:T(8,128)(2,1)}, bf16[512,1024]{1,0:T(8,128)(2,1)}, u32[]{:S(2)}, u32[]{:S(2)}) collective-permute-start(bf16[512,1024]{1,0:T(8,128)(2,1)} %convolution_convert_fusion.2), channel_id=1, source_target_pairs={{0,1},{1,0},{2,3},{3,2},{4,5},{5,4},{6,7},{7,6},{8,9},{9,8},{10,11... | collective-permute-start | bytes 3145736 | tf_op jit(solution)/shard_map/ppermute | solution.py:22
  52.2 50.2 %copy-start.8 = (f32[4096]{0:T(1024)S(1)}, f32[4096]{0:T(1024)}, u32[]{:S(2)}) copy-start(f32[4096]{0:T(1024)} %param.16) | copy-start | bytes 49156
  91.1 7.1 %collective-permute-start.12 = (bf16[16,1024]{1,0:T(8,128)(2,1)S(1)}, bf16[16,1024]{1,0:T(8,128)(2,1)S(1)}, u32[]{:S(2)}, u32[]{:S(2)}) collective-permute-start(bf16[16,1024]{1,0:T(8,128)(2,1)S(1)} %get-tuple-element.36), channel_id=1, source_target_pairs={{0,48},{16,0},{32,16},{48,32},{64,112},{80,64},{96,80},{112,96},{1... | collective-permute-start | bytes 98312 | tf_op jit(solution)/shard_map/ppermute | solution.py:31
  95.2 5.4 %collective-permute-start.11 = (bf16[16,1024]{1,0:T(8,128)(2,1)S(1)}, bf16[16,1024]{1,0:T(8,128)(2,1)S(1)}, u32[]{:S(2)}, u32[]{:S(2)}) collective-permute-start(bf16[16,1024]{1,0:T(8,128)(2,1)S(1)} %get-tuple-element.37), channel_id=1, source_target_pairs={{0,32},{16,48},{32,0},{48,16},{64,96},{80,112},{96,64},{112,80},{1... | collective-permute-start | bytes 98312 | tf_op jit(solution)/shard_map/ppermute | solution.py:31
  96.9 4.0 %collective-permute-start.10 = (bf16[16,1024]{1,0:T(8,128)(2,1)S(1)}, bf16[16,1024]{1,0:T(8,128)(2,1)S(1)}, u32[]{:S(2)}, u32[]{:S(2)}) collective-permute-start(bf16[16,1024]{1,0:T(8,128)(2,1)S(1)} %get-tuple-element.38), channel_id=1, source_target_pairs={{0,16},{16,32},{32,48},{48,0},{64,80},{80,96},{96,112},{112,64},{1... | collective-permute-start | bytes 98312 | tf_op jit(solution)/shard_map/ppermute | solution.py:31
  132.3 42.4 %copy-start.11 = (bf16[1,4096,384]{2,1,0:T(8,128)(2,1)S(1)}, bf16[1,4096,384]{2,1,0:T(8,128)(2,1)}, u32[]{:S(2)}) copy-start(bf16[1,4096,384]{2,1,0:T(8,128)(2,1)} %param.19) | copy-start | bytes 9437188
  174.7 2.6 copy-start.1
  (1 other events, 0.7 us)

commit v3 on v2

--- a/solution.py
+++ b/solution.py
@@ -3,6 +3,8 @@
 import jax
 import jax.numpy as jnp
 from jax import lax
+from jax.experimental import pallas as pl
+from jax.experimental.pallas import tpu as pltpu
 from jax.sharding import PartitionSpec as P
 
 HEADS = 64
@@ -40,6 +42,77 @@
     return lax.all_to_all(
         array, "tensor", split_axis=0, concat_axis=0, tiled=True, axis_index_groups=groups
     )
+
+
+def experts_kernel(rows, gate_a, up_a, gate_b, up_b, down_a, down_b, out, wide, tall, total, inner, wide_sems, tall_sems):
+    hidden = gate_a.shape[1]
+    depth = rows.shape[1]
+    steps = wide_sems.shape[0]
+    chunk = depth // steps
+
+    def wide_copy(step, place):
+        span = pl.ds(pl.multiple_of(step * chunk, chunk), chunk)
+        source = (gate_a, gate_b, up_a, up_b)[place]
+        target = wide.at[span, pl.ds(place * hidden, hidden)]
+        return pltpu.make_async_copy(source.at[span, :], target, wide_sems.at[step, place])
+
+    def tall_copy(place):
+        target = tall.at[pl.ds(place * hidden, hidden), :]
+        return pltpu.make_async_copy((down_a, down_b)[place], target, tall_sems.at[place])
+
+    for step in range(steps):
+        for place in range(4):
+            wide_copy(step, place).start()
+    for place in range(2):
+        tall_copy(place).start()
+    total[...] = jnp.zeros_like(total)
+
+    def multiply(step, carry):
+        for place in range(4):
+            wide_copy(step, place).wait()
+        span = pl.ds(pl.multiple_of(step * chunk, chunk), chunk)
+        total[...] += jnp.dot(rows[:, span], wide[span, :], preferred_element_type=F32)
+        return carry
+
+    lax.fori_loop(0, steps, multiply, 0)
+    value = total[:, : 2 * hidden]
+    inner[...] = (value / (1.0 + jnp.exp(-value)) * total[:, 2 * hidden :]).astype(BF16)
+    for place in range(2):
+        tall_copy(place).wait()
+
+    def project(step, carry):
+        span = pl.ds(pl.multiple_of(step * chunk, chunk), chunk)
+        out[:, span] = jnp.dot(inner[...], tall[:, span], preferred_element_type=F32).astype(BF16)
+        return carry
+
+    lax.fori_loop(0, steps, project, 0)
+
+
+def experts(rows, gate_a, up_a, down_a, gate_b, up_b, down_b):
+    count, depth = rows.shape
+    hidden = gate_a.shape[1]
+    steps = 4
+    whole = pl.BlockSpec(memory_space=pltpu.VMEM)
+    return pl.pallas_call(
+        experts_kernel,
+        in_specs=[whole] + [pl.BlockSpec(memory_space=pl.ANY)] * 6,
+        out_specs=whole,
+        out_shape=jax.ShapeDtypeStruct((count, depth), BF16),
+        scratch_shapes=[
+            pltpu.VMEM((depth, 4 * hidden), BF16),
+            pltpu.VMEM((2 * hidden, depth), BF16),
+            pltpu.VMEM((count, 4 * hidden), F32),
+            pltpu.VMEM((count, 2 * hidden), BF16),
+            pltpu.SemaphoreType.DMA((steps, 4)),
+            pltpu.SemaphoreType.DMA((2,)),
+        ],
+        compiler_params=pltpu.CompilerParams(vmem_limit_bytes=44 * 1024 * 1024),
+        cost_estimate=pl.CostEstimate(
+            flops=12 * count * depth * hidden,
+            bytes_accessed=12 * hidden * depth + 4 * count * depth,
+            transcendentals=2 * count * hidden,
+        ),
+    )(rows, gate_a, up_a, gate_b, up_b, down_a, down_b)
 
 
 def attend(queries, keys_values, prefix_len, kv_index):
@@ -116,9 +189,11 @@
     place_y, place_x = expert_index // side_x, expert_index % side_x
     part_width = out_proj.shape[1]
     blocks = [out_proj] + [shift(out_proj, d, 0, side_y, side_x) for d in range(1, side_y)]
+    attended = attend(queries, keys_values, prefix_len, tensor_index * per_device // (HEADS // KVH))
+    attended, blocks, gate_other, up_other, down_other = lax.optimization_barrier(
+        (attended, blocks, gate_other, up_other, down_other)
+    )
     projection = jnp.concatenate(ordered(blocks, place_y), axis=1)
-
-    attended = attend(queries, keys_values, prefix_len, tensor_index * per_device // (HEADS // KVH))
     attended = attended.reshape(chips, 2, TOK_DEV, per_device * HD)
     attended = [lax.dynamic_index_in_dim(attended, c, 1, keepdims=False) for c in (1 - core, core)]
     attended = jnp.stack(attended).reshape(2, half_rows, per_device * HD)
@@ -131,8 +206,8 @@
     chip_part = (part_here.astype(F32) + part_away.astype(F32)).astype(BF16)
     chip_part = chip_part.reshape(side_x, chips, TOK_DEV, side_y * part_width)
     chip_part = jnp.transpose(chip_part, (1, 0, 2, 3))
-    chip_part, pick, combine, gate_other, up_other, down_other, residual, norm_gain = lax.optimization_barrier(
-        (chip_part, pick, combine, gate_other, up_other, down_other, residual, norm_gain)
+    chip_part, pick, combine, residual, norm_gain = lax.optimization_barrier(
+        (chip_part, pick, combine, residual, norm_gain)
     )
     head_parts = along_z(chip_part, same_core)
     sums = jnp.sum(head_parts.astype(F32), axis=0).astype(BF16)
@@ -153,14 +228,8 @@
     )
     rows = arrived.reshape(expert_count * capacity, width)
 
-    def inner_of(gate, up):
-        gate_val = jnp.dot(rows, gate, preferred_element_type=F32)
-        up_val = jnp.dot(rows, up, preferred_element_type=F32)
-        return (jax.nn.silu(gate_val) * up_val).astype(BF16)
-
-    result = jnp.dot(inner_of(w_gate[0], w_up[0]), w_down[0], preferred_element_type=F32)
-    result = result + jnp.dot(inner_of(gate_other, up_other), down_other, preferred_element_type=F32)
-    result = result.astype(BF16).reshape(expert_count, capacity, width)
+    result = experts(rows, w_gate[0], w_up[0], w_down[0], gate_other, up_other, down_other)
+    result = result.reshape(expert_count, capacity, width)
     returned = lax.all_to_all(result, "expert", split_axis=0, concat_axis=0, tiled=True)
     expert_part = jnp.dot(combine, returned.reshape(expert_count * capacity, width), preferred_element_type=F32)
     expert_parts = along_z(expert_part.astype(BF16).reshape(chips, TOK_DEV, width), same_core)

time: 273 us -> 247 us (0.905)
  matrix products: 41.1 us -> 13.9 us
  Pallas kernels: 0 us -> 10.8 us
  waiting for transfers between devices: 20.1 us -> 15.5 us
  local copies, waits for them, and re-layouts: 7.68 us -> 3.96 us
    dot_general x4 -> x0, matrix products: 27 us -> none  [the longest x1 10.7 us: shards(): jnp.dot(inner_of(gate_other, up_other), down_other, preferred_element_typ...]
    pallas_call x0 -> x1, Pallas kernels: none -> 10.8 us  [experts(): pl.pallas_call(experts_kernel, in_specs=[whole] + [pl.BlockSpec(memory_sp...]
    ppermute x9, waiting for transfers between devices: 19.1 us -> 14.5 us  [shift(): return lax.ppermute(array, 'expert', pairs)]
    squeeze x3, local copies, waits for them, and re-layouts: 4.26 us -> 0.71 us  [shards(): rows_here = jnp.concatenate([piece[1] for piece in pieces], axis=0)]
  transfers between devices with their start and end apart: 13 -> 13, of which waited for: 7 -> 6; matrix products, arithmetic and copies ran while one was open for 8% -> 5% of each run, Pallas kernels for 0% -> 0%
where the time goes in v3:
time: 247 us; the launch traced here: 246 us
  blocking collectives  177 us (72%)
  starting transfers between devices  17.1 us (7%)
  waiting for transfers between devices  15.5 us (6%)
  matrix products  13.9 us (6%)
  Pallas kernels  10.8 us (4%)
  other arithmetic  6.8 us (3%)
  local copies, waits for them, and re-layouts  3.96 us (2%)
    all_to_all x3, blocking collectives, along_z(): lax.all_to_all(array, 'tensor', split_axis=0, concat_axis=0, tiled=True,...  97 us
    all_to_all x1, blocking collectives, shards(): lax.all_to_all(outgoing.reshape(expert_count, capacity, width), 'expert',...  43.3 us
    all_to_all x1, blocking collectives, shards(): lax.all_to_all(result, 'expert', split_axis=0, concat_axis=0, tiled=True)  36.8 us
    ppermute x9, starting transfers between devices, shift(): return lax.ppermute(array, 'expert', pairs)  16.3 us
    ppermute x9, waiting for transfers between devices, shift(): return lax.ppermute(array, 'expert', pairs)  14.5 us
    pallas_call x1, Pallas kernels, experts(): pl.pallas_call(experts_kernel, in_specs=[whole] + [pl.BlockSpec(memory_sp...  10.8 us
    sub x1, matrix products, attend(): weights = jnp.exp(jnp.where(visible, scores - highest, -1e+30))  5.02 us
  transfers between devices with their start and end apart: 13, of which 6 were waited for; matrix products, arithmetic and copies ran while one was open for 5% of the time, Pallas kernels for 0%

profile of v3, /device:TPU:2, one launch (start us, length us, event | category | flops | bytes accessed | tf_op | source)
XLA Modules:
  0.0 246.3 jit_solution(3237246514104237564)
XLA Ops:
  0.6 3.2 %collective-permute-start.1 = (bf16[512,256]{1,0:T(8,128)(2,1)}, bf16[512,256]{1,0:T(8,128)(2,1)}, u32[]{:S(2)}, u32[]{:S(2)}) collective-permute-start(bf16[512,256]{1,0:T(8,128)(2,1)} %param.14), channel_id=1, source_target_pairs={{0,128},{16,144},{32,160},{48,176},{64,192},{80,208},{96,224},{112... | collective-permute-start | bytes 786440 | tf_op jit(solution)/shard_map/ppermute | solution.py:33
  5.2 2.0 fusion.11
  7.3 5.0 %fusion.67 = (f32[4,256]{1,0:T(4,128)S(1)}, bf16[4,256,1280]{1,2,0:T(8,128)(2,1)}) fusion(pred[256,1280]{0,1:T(8,128)(4,1)} %fusion.11, bf16[1280,256]{1,0:T(8,128)(2,1)S(1)} %dynamic-slice_bitcast_fusion, bf16[256,512]{1,0:T(8,128)(2,1)} %param.11), kind=kOutput, calls=%fused_computation.111 | convolution fusion | flops 680264960 | bytes 4460544 | tf_op jit(solution)/shard_map/sub | solution.py:131
  12.3 2.6 %collective-permute-start.2 = (bf16[512,256]{1,0:T(8,128)(2,1)S(1)}, bf16[512,256]{1,0:T(8,128)(2,1)S(1)}, u32[]{:S(2)}, u32[]{:S(2)}) collective-permute-start(bf16[512,256]{1,0:T(8,128)(2,1)S(1)} %copy-done.2), channel_id=1, source_target_pairs={{0,192},{16,208},{32,224},{48,240},{64,0},{80,16},{96,32},{112,48}... | collective-permute-start | bytes 786440 | tf_op jit(solution)/shard_map/ppermute | solution.py:33
  14.9 3.0 %fusion.18 = bf16[256,4,128]{0,2,1:T(8,128)(2,1)} fusion(bf16[4,256,1280]{1,2,0:T(8,128)(2,1)} %get-tuple-element.58, bf16[1280,256]{1,0:T(8,128)(2,1)S(1)} %dynamic-slice_bitcast_fusion, f32[256,4]{0,1:T(4,128)S(1)} %bitcast.154), kind=kOutput, calls=%fused_computation.23 | convolution fusion | flops 335806464 | bytes 3215360 | tf_op jit(solution)/shard_map/hnc,cd->nhd/dot_general | solution.py:133
  18.0 2.6 %collective-permute-done.2 = bf16[512,256]{1,0:T(8,128)(2,1)S(1)} collective-permute-done((bf16[512,256]{1,0:T(8,128)(2,1)S(1)}, bf16[512,256]{1,0:T(8,128)(2,1)S(1)}, u32[]{:S(2)}, u32[]{:S(2)}) %collective-permute-start.2) | collective-permute-done | bytes 262176 | tf_op jit(solution)/shard_map/ppermute | solution.py:33
  21.3 1.1 copy.59
  23.3 2.2 collective-permute-start.7
  25.4 1.8 collective-permute-start.6
  27.2 1.2 select_select_fusion.3
  28.5 2.4 collective-permute-done.8
  30.9 5.4 %collective-permute-done.7 = bf16[2,128,512]{2,1,0:T(8,128)(2,1)S(1)} collective-permute-done((bf16[2,128,512]{2,1,0:T(8,128)(2,1)S(1)}, bf16[2,128,512]{2,1,0:T(8,128)(2,1)S(1)}, u32[]{:S(2)}, u32[]{:S(2)}) %collective-permute-start.7) | collective-permute-done | bytes 262176 | tf_op jit(solution)/shard_map/ppermute | solution.py:33
  37.9 1.7 convolution_convert_fusion.2
  42.8 2.3 add_convert_fusion
  45.2 37.5 %all_to_all.25 = bf16[8,4,16,1024]{3,2,1,0:T(8,128)(2,1)} all-to-all(bf16[8,4,16,1024]{3,2,1,0:T(8,128)(2,1)S(1)} %bitcast.136), channel_id=1, replica_groups={{0,2,4,6,8,10,12,14},{1,3,5,7,9,11,13,15},{16,18,20,22,24,26,28,30},{17..., dimensions={0} | all-to-all | bytes 2097152 | tf_op jit(solution)/shard_map/all_to_all | solution.py:42
  82.7 1.4 reduce_sum.60
  84.1 2.8 %collective-permute-start.12 = (bf16[16,1024]{1,0:T(8,128)(2,1)S(1)}, bf16[16,1024]{1,0:T(8,128)(2,1)S(1)}, u32[]{:S(2)}, u32[]{:S(2)}) collective-permute-start(bf16[16,1024]{1,0:T(8,128)(2,1)S(1)} %get-tuple-element.46), channel_id=1, source_target_pairs={{0,48},{16,0},{32,16},{48,32},{64,112},{80,64},{96,80},{112,96},{1... | collective-permute-start | bytes 98312 | tf_op jit(solution)/shard_map/ppermute | solution.py:33
  87.1 2.0 collective-permute-start.10
  89.1 3.2 %collective-permute-done.11 = bf16[16,1024]{1,0:T(8,128)(2,1)S(1)} collective-permute-done((bf16[16,1024]{1,0:T(8,128)(2,1)S(1)}, bf16[16,1024]{1,0:T(8,128)(2,1)S(1)}, u32[]{:S(2)}, u32[]{:S(2)}) %collective-permute-start.11) | collective-permute-done | bytes 32800 | tf_op jit(solution)/shard_map/ppermute | solution.py:33
  93.3 28.9 %all_to_all.26 = bf16[8,16,4096]{2,1,0:T(8,128)(2,1)S(1)} all-to-all(bf16[8,16,4096]{2,1,0:T(8,128)(2,1)S(1)} %broadcast_in_dim.79), channel_id=1, replica_groups={{0,2,4,6,8,10,12,14},{1,3,5,7,9,11,13,15},{16,18,20,22,24,26,28,30},{17..., dimensions={0} | all-to-all | bytes 2097152 | tf_op jit(solution)/shard_map/all_to_all | solution.py:42
  123.2 43.3 %all_to_all.27 = bf16[16,24,4096]{2,1,0:T(8,128)(2,1)S(1)} all-to-all(bf16[16,24,4096]{2,1,0:T(8,128)(2,1)S(1)} %bitcast.134), channel_id=1, replica_groups=mesh['expert'=16,'tensor'=16] {'expert'}, dimensions={0} | all-to-all | bytes 6291456 | tf_op jit(solution)/shard_map/all_to_all | solution.py:226
  166.5 10.8 %shard_map.109 = bf16[384,4096]{1,0:T(8,128)(2,1)S(1)} custom-call(bf16[384,4096]{1,0:T(8,128)(2,1)S(1)} %bitcast.130, bf16[4096,384]{1,0:T(8,128)(2,1)S(1)} %bitcast.133, bf16[4096,384]{1,0:T(8,128)(2,1)} %bitcast.151, bf16[4096,384]{1,0:T(8,128)(2,1)} %collective-permute-done.3.gate_b, bf16[4096,384]{1,0:T(8,128)(2,1)} %collective-permute-done.4.up_b, ...), custom_call_target="tpu_custom_call" | custom-call | flops 7247757312 | bytes 25165824 | tf_op jit(solution)/shard_map/pallas_call | solution.py:96
  177.4 36.8 %all_to_all.28 = bf16[16,24,4096]{2,1,0:T(8,128)(2,1)S(1)} all-to-all(bf16[16,24,4096]{2,1,0:T(8,128)(2,1)S(1)} %bitcast.131), channel_id=1, replica_groups=mesh['expert'=16,'tensor'=16] {'expert'}, dimensions={0} | all-to-all | bytes 6291456 | tf_op jit(solution)/shard_map/all_to_all | solution.py:233
  214.9 30.6 %all_to_all.29 = bf16[8,16,4096]{2,1,0:T(8,128)(2,1)S(1)} all-to-all(bf16[8,16,4096]{2,1,0:T(8,128)(2,1)S(1)} %bitcast.138), channel_id=1, replica_groups={{0,2,4,6,8,10,12,14},{1,3,5,7,9,11,13,15},{16,18,20,22,24,26,28,30},{17..., dimensions={0} | all-to-all | bytes 2097152 | tf_op jit(solution)/shard_map/all_to_all | solution.py:42
  (86 shorter events, 11.4 us)
Async XLA Ops:
  0.0 5.2 %copy-start = (bf16[1,4,1280,256]{3,2,1,0:T(8,128)(2,1)S(1)}, bf16[1,4,1280,256]{3,2,1,0:T(8,128)(2,1)}, u32[]{:S(2)}) copy-start(bf16[1,4,1280,256]{3,2,1,0:T(8,128)(2,1)} %param.12) | copy-start | bytes 7864324
  0.0 20.6 %collective-permute-start.3 = (bf16[4096,384]{1,0:T(8,128)(2,1)}, bf16[4096,384]{1,0:T(8,128)(2,1)}, u32[]{:S(2)}, u32[]{:S(2)}) collective-permute-start(bf16[4096,384]{1,0:T(8,128)(2,1)} %bitcast.132), channel_id=1, source_target_pairs={{0,1},{1,0},{2,3},{3,2},{4,5},{5,4},{6,7},{7,6},{8,9},{9,8},{10,11... | collective-permute-start | bytes 9437192 | tf_op jit(solution)/shard_map/ppermute | solution.py:24
  0.0 20.6 %collective-permute-start.4 = (bf16[4096,384]{1,0:T(8,128)(2,1)}, bf16[4096,384]{1,0:T(8,128)(2,1)}, u32[]{:S(2)}, u32[]{:S(2)}) collective-permute-start(bf16[4096,384]{1,0:T(8,128)(2,1)} %bitcast.150), channel_id=1, source_target_pairs={{0,1},{1,0},{2,3},{3,2},{4,5},{5,4},{6,7},{7,6},{8,9},{9,8},{10,11... | collective-permute-start | bytes 9437192 | tf_op jit(solution)/shard_map/ppermute | solution.py:24
  0.5 20.1 %collective-permute-start.5 = (bf16[384,4096]{1,0:T(8,128)(2,1)}, bf16[384,4096]{1,0:T(8,128)(2,1)}, u32[]{:S(2)}, u32[]{:S(2)}) collective-permute-start(bf16[384,4096]{1,0:T(8,128)(2,1)} %bitcast.152), channel_id=1, source_target_pairs={{0,1},{1,0},{2,3},{3,2},{4,5},{5,4},{6,7},{7,6},{8,9},{9,8},{10,11... | collective-permute-start | bytes 9437192 | tf_op jit(solution)/shard_map/ppermute | solution.py:24
  0.6 11.7 %collective-permute-start.1 = (bf16[512,256]{1,0:T(8,128)(2,1)}, bf16[512,256]{1,0:T(8,128)(2,1)}, u32[]{:S(2)}, u32[]{:S(2)}) collective-permute-start(bf16[512,256]{1,0:T(8,128)(2,1)} %param.14), channel_id=1, source_target_pairs={{0,128},{16,144},{32,160},{48,176},{64,192},{80,208},{96,224},{112... | collective-permute-start | bytes 786440 | tf_op jit(solution)/shard_map/ppermute | solution.py:33
  3.8 14.1 %collective-permute-start = (bf16[512,256]{1,0:T(8,128)(2,1)}, bf16[512,256]{1,0:T(8,128)(2,1)}, u32[]{:S(2)}, u32[]{:S(2)}) collective-permute-start(bf16[512,256]{1,0:T(8,128)(2,1)} %param.14), channel_id=1, source_target_pairs={{0,64},{16,80},{32,96},{48,112},{64,128},{80,144},{96,160},{112,17... | collective-permute-start | bytes 786440 | tf_op jit(solution)/shard_map/ppermute | solution.py:33
  7.3 5.0 %copy-start.2 = (bf16[512,256]{1,0:T(8,128)(2,1)S(1)}, bf16[512,256]{1,0:T(8,128)(2,1)}, u32[]{:S(2)}) copy-start(bf16[512,256]{1,0:T(8,128)(2,1)} %param.14) | copy-start | bytes 786436
  12.3 8.2 %collective-permute-start.2 = (bf16[512,256]{1,0:T(8,128)(2,1)S(1)}, bf16[512,256]{1,0:T(8,128)(2,1)S(1)}, u32[]{:S(2)}, u32[]{:S(2)}) collective-permute-start(bf16[512,256]{1,0:T(8,128)(2,1)S(1)} %copy-done.2), channel_id=1, source_target_pairs={{0,192},{16,208},{32,224},{48,240},{64,0},{80,16},{96,32},{112,48}... | collective-permute-start | bytes 786440 | tf_op jit(solution)/shard_map/ppermute | solution.py:33
  20.6 0.7 copy-start.6
  22.4 8.4 %collective-permute-start.8 = (bf16[2,128,512]{2,1,0:T(8,128)(2,1)S(1)}, bf16[2,128,512]{2,1,0:T(8,128)(2,1)S(1)}, u32[]{:S(2)}, u32[]{:S(2)}) collective-permute-start(bf16[2,128,512]{2,1,0:T(8,128)(2,1)S(1)} %pad_maximum_fusion.1), channel_id=1, source_target_pairs={{0,48},{16,0},{32,16},{48,32},{64,112},{80,64},{96,80},{112,96},{1... | collective-permute-start | bytes 786440 | tf_op jit(solution)/shard_map/ppermute | solution.py:33
  23.3 13.0 %collective-permute-start.7 = (bf16[2,128,512]{2,1,0:T(8,128)(2,1)S(1)}, bf16[2,128,512]{2,1,0:T(8,128)(2,1)S(1)}, u32[]{:S(2)}, u32[]{:S(2)}) collective-permute-start(bf16[2,128,512]{2,1,0:T(8,128)(2,1)S(1)} %pad_maximum_fusion.1), channel_id=1, source_target_pairs={{0,32},{16,48},{32,0},{48,16},{64,96},{80,112},{96,64},{112,80},{1... | collective-permute-start | bytes 786440 | tf_op jit(solution)/shard_map/ppermute | solution.py:33
  25.4 11.7 %collective-permute-start.6 = (bf16[2,128,512]{2,1,0:T(8,128)(2,1)S(1)}, bf16[2,128,512]{2,1,0:T(8,128)(2,1)S(1)}, u32[]{:S(2)}, u32[]{:S(2)}) collective-permute-start(bf16[2,128,512]{2,1,0:T(8,128)(2,1)S(1)} %pad_maximum_fusion.1), channel_id=1, source_target_pairs={{0,16},{16,32},{32,48},{48,0},{64,80},{80,96},{96,112},{112,64},{1... | collective-permute-start | bytes 786440 | tf_op jit(solution)/shard_map/ppermute | solution.py:33
  28.5 11.1 %copy-start.3 = (bf16[512,256]{1,0:T(8,128)(2,1)}, bf16[512,256]{1,0:T(8,128)(2,1)S(1)}, u32[]{:S(2)}) copy-start(bf16[512,256]{1,0:T(8,128)(2,1)S(1)} %get-tuple-element.34) | copy-start | bytes 786436
  28.5 11.1 %copy-start.4 = (bf16[512,256]{1,0:T(8,128)(2,1)}, bf16[512,256]{1,0:T(8,128)(2,1)S(1)}, u32[]{:S(2)}) copy-start(bf16[512,256]{1,0:T(8,128)(2,1)S(1)} %get-tuple-element.35) | copy-start | bytes 786436
  28.5 11.1 %copy-start.5 = (bf16[512,256]{1,0:T(8,128)(2,1)}, bf16[512,256]{1,0:T(8,128)(2,1)S(1)}, u32[]{:S(2)}) copy-start(bf16[512,256]{1,0:T(8,128)(2,1)S(1)} %get-tuple-element.36) | copy-start | bytes 786436
  37.8 2.1 copy-start.10
  37.8 2.3 copy-start.9
  39.6 3.3 %collective-permute-start.9 = (bf16[512,1024]{1,0:T(8,128)(2,1)}, bf16[512,1024]{1,0:T(8,128)(2,1)}, u32[]{:S(2)}, u32[]{:S(2)}) collective-permute-start(bf16[512,1024]{1,0:T(8,128)(2,1)} %convolution_convert_fusion.2), channel_id=1, source_target_pairs={{0,1},{1,0},{2,3},{3,2},{4,5},{5,4},{6,7},{7,6},{8,9},{9,8},{10,11... | collective-permute-start | bytes 3145736 | tf_op jit(solution)/shard_map/ppermute | solution.py:24
  45.2 47.7 %copy-start.7 = (bf16[16,4096]{1,0:T(8,128)(2,1)S(1)}, bf16[16,4096]{1,0:T(8,128)(2,1)}, u32[]{:S(2)}) copy-start(bf16[16,4096]{1,0:T(8,128)(2,1)} %param.15) | copy-start | bytes 393220
  82.7 10.4 %copy-start.8 = (f32[4096]{0:T(1024)S(1)}, f32[4096]{0:T(1024)}, u32[]{:S(2)}) copy-start(f32[4096]{0:T(1024)} %param.16) | copy-start | bytes 49156
  84.1 5.0 %collective-permute-start.12 = (bf16[16,1024]{1,0:T(8,128)(2,1)S(1)}, bf16[16,1024]{1,0:T(8,128)(2,1)S(1)}, u32[]{:S(2)}, u32[]{:S(2)}) collective-permute-start(bf16[16,1024]{1,0:T(8,128)(2,1)S(1)} %get-tuple-element.46), channel_id=1, source_target_pairs={{0,48},{16,0},{32,16},{48,32},{64,112},{80,64},{96,80},{112,96},{1... | collective-permute-start | bytes 98312 | tf_op jit(solution)/shard_map/ppermute | solution.py:33
  86.9 5.4 %collective-permute-start.11 = (bf16[16,1024]{1,0:T(8,128)(2,1)S(1)}, bf16[16,1024]{1,0:T(8,128)(2,1)S(1)}, u32[]{:S(2)}, u32[]{:S(2)}) collective-permute-start(bf16[16,1024]{1,0:T(8,128)(2,1)S(1)} %get-tuple-element.47), channel_id=1, source_target_pairs={{0,32},{16,48},{32,0},{48,16},{64,96},{80,112},{96,64},{112,80},{1... | collective-permute-start | bytes 98312 | tf_op jit(solution)/shard_map/ppermute | solution.py:33
  87.1 5.3 %collective-permute-start.10 = (bf16[16,1024]{1,0:T(8,128)(2,1)S(1)}, bf16[16,1024]{1,0:T(8,128)(2,1)S(1)}, u32[]{:S(2)}, u32[]{:S(2)}) collective-permute-start(bf16[16,1024]{1,0:T(8,128)(2,1)S(1)} %get-tuple-element.48), channel_id=1, source_target_pairs={{0,16},{16,32},{32,48},{48,0},{64,80},{80,96},{96,112},{112,64},{1... | collective-permute-start | bytes 98312 | tf_op jit(solution)/shard_map/ppermute | solution.py:33
  123.2 43.3 %copy-start.1 = (bf16[1,4096,384]{2,1,0:T(8,128)(2,1)S(1)}, bf16[1,4096,384]{2,1,0:T(8,128)(2,1)}, u32[]{:S(2)}) copy-start(bf16[1,4096,384]{2,1,0:T(8,128)(2,1)} %param.19) | copy-start | bytes 9437188

commit v4 on v3

--- a/solution.py
+++ b/solution.py
@@ -115,24 +115,58 @@
     )(rows, gate_a, up_a, gate_b, up_b, down_a, down_b)
 
 
-def attend(queries, keys_values, prefix_len, kv_index):
-    step_rows = queries.shape[0]
-    per_device = queries.shape[1] // HD
-    cached = lax.dynamic_index_in_dim(keys_values[0], kv_index, 0, keepdims=False)
-    key_rows = cached[:, :HD]
-    value_rows = cached[:, HD:]
-    context = cached.shape[0]
-    query_rows = queries.reshape(step_rows, per_device, HD)
-    scores = jnp.einsum("nhd,cd->hnc", query_rows, key_rows, preferred_element_type=F32) / math.sqrt(HD)
-    columns = jnp.arange(context, dtype=jnp.int32)[None, :]
-    positions = jnp.arange(step_rows, dtype=jnp.int32)[:, None]
-    visible = ((columns < prefix_len[0]) | (columns >= PREFIX) & (columns - PREFIX <= positions))[None]
-    highest = jnp.max(jnp.where(visible, scores, -1e30), axis=-1, keepdims=True)
-    weights = jnp.exp(jnp.where(visible, scores - highest, -1e30))
-    summed = jnp.sum(weights, axis=-1)
-    blended = jnp.einsum("hnc,cd->nhd", weights.astype(BF16), value_rows, preferred_element_type=F32)
-    attended = (blended / jnp.transpose(summed)[:, :, None]).astype(BF16)
-    return attended.reshape(step_rows, per_device * HD)
+def attend_kernel(scalars, queries, cached, out):
+    rows = queries.shape[0]
+    key, value = cached[0, 0, :, :HD], cached[0, 0, :, HD:]
+    old_column = lax.broadcasted_iota(jnp.int32, (1, PREFIX), 1)
+    live = old_column < scalars[1]
+    step = (rows, key.shape[0] - PREFIX)
+    causal = lax.broadcasted_iota(jnp.int32, step, 1) <= lax.broadcasted_iota(jnp.int32, step, 0)
+    scale = 1.0 / (math.log(2.0) * math.sqrt(HD))
+    contract = (((1,), (1,)), ((), ()))
+    for head in range(queries.shape[1] // HD):
+        span = slice(head * HD, (head + 1) * HD)
+        query = queries[:, span]
+        old = lax.dot_general(query, key[:PREFIX], contract, preferred_element_type=F32)
+        new = lax.dot_general(query, key[PREFIX:], contract, preferred_element_type=F32)
+        old = jnp.where(live, old, -1e30)
+        new = jnp.where(causal, new, -1e30)
+        highest = jnp.maximum(jnp.max(old, axis=-1, keepdims=True), jnp.max(new, axis=-1, keepdims=True))
+        old = jnp.exp2((old - highest) * scale)
+        new = jnp.exp2((new - highest) * scale)
+        total = jnp.sum(old, axis=-1, keepdims=True) + jnp.sum(new, axis=-1, keepdims=True)
+        blended = jnp.dot(old.astype(BF16), value[:PREFIX], preferred_element_type=F32)
+        blended = blended + jnp.dot(new.astype(BF16), value[PREFIX:], preferred_element_type=F32)
+        attended = (blended / total).reshape(rows // (2 * TOK_DEV), 2, TOK_DEV, HD)
+        even, odd = attended[:, 0], attended[:, 1]
+        first = scalars[2] == 0
+        out[0, :, :, span] = jnp.where(first, odd, even).astype(BF16)
+        out[1, :, :, span] = jnp.where(first, even, odd).astype(BF16)
+
+
+def attend(scalars, queries, keys_values):
+    rows, width = queries.shape
+    context = keys_values.shape[2]
+    shape = (2, rows // (2 * TOK_DEV), TOK_DEV, width)
+    return pl.pallas_call(
+        attend_kernel,
+        grid_spec=pltpu.PrefetchScalarGridSpec(
+            num_scalar_prefetch=1,
+            grid=(1,),
+            in_specs=[
+                pl.BlockSpec((rows, width), lambda s, scalars: (0, 0)),
+                pl.BlockSpec((1, 1, context, 2 * HD), lambda s, scalars: (0, scalars[0], 0, 0)),
+            ],
+            out_specs=pl.BlockSpec(shape, lambda s, scalars: (0, 0, 0, 0)),
+        ),
+        out_shape=jax.ShapeDtypeStruct(shape, BF16),
+        compiler_params=pltpu.CompilerParams(vmem_limit_bytes=40 * 1024 * 1024),
+        cost_estimate=pl.CostEstimate(
+            flops=4 * rows * width * context,
+            bytes_accessed=4 * rows * width + 4 * context * HD,
+            transcendentals=rows * (width // HD) * context,
+        ),
+    )(scalars, queries, keys_values)
 
 
 def shards(
@@ -158,10 +192,6 @@
     width = residual.shape[1]
     half_rows = chips * TOK_DEV
 
-    gate_other = chip_swap(w_gate[0], tensor_count)
-    up_other = chip_swap(w_up[0], tensor_count)
-    down_other = chip_swap(w_down[0], tensor_count)
-
     slot_index = tensor_index // HSPLIT
     slot_count = tensor_count // HSPLIT
     capacity = chips * MOST
@@ -189,26 +219,29 @@
     place_y, place_x = expert_index // side_x, expert_index % side_x
     part_width = out_proj.shape[1]
     blocks = [out_proj] + [shift(out_proj, d, 0, side_y, side_x) for d in range(1, side_y)]
-    attended = attend(queries, keys_values, prefix_len, tensor_index * per_device // (HEADS // KVH))
-    attended, blocks, gate_other, up_other, down_other = lax.optimization_barrier(
-        (attended, blocks, gate_other, up_other, down_other)
-    )
+    kv_index = tensor_index * per_device // (HEADS // KVH)
+    scalars = jnp.stack([kv_index, prefix_len[0], core]).astype(jnp.int32)
+    scalars, gate_own, up_own, down_own = lax.optimization_barrier((scalars, w_gate[0], w_up[0], w_down[0]))
+    gate_other = chip_swap(gate_own, tensor_count)
+    up_other = chip_swap(up_own, tensor_count)
+    attended = attend(scalars, queries, keys_values)
+    attended, blocks, gate_other, up_other, down_own = lax.optimization_barrier(
+        (attended, blocks, gate_other, up_other, down_own)
+    )
+    down_other = chip_swap(down_own, tensor_count)
     projection = jnp.concatenate(ordered(blocks, place_y), axis=1)
-    attended = attended.reshape(chips, 2, TOK_DEV, per_device * HD)
-    attended = [lax.dynamic_index_in_dim(attended, c, 1, keepdims=False) for c in (1 - core, core)]
-    attended = jnp.stack(attended).reshape(2, half_rows, per_device * HD)
     pieces = [attended] + [shift(attended, 0, d, side_y, side_x) for d in range(1, side_x)]
-    rows_away = jnp.concatenate([piece[0] for piece in pieces], axis=0)
-    rows_here = jnp.concatenate([piece[1] for piece in pieces], axis=0)
+    pieces, projection, pick, combine, down_other = lax.optimization_barrier(
+        (pieces, projection, pick, combine, down_other)
+    )
+    rows_away = jnp.stack([piece[0] for piece in pieces], axis=1).reshape(-1, per_device * HD)
+    rows_here = jnp.stack([piece[1] for piece in pieces], axis=1).reshape(-1, per_device * HD)
     part_away = jnp.dot(rows_away, projection, preferred_element_type=F32).astype(BF16)
     part_away = chip_swap(part_away, tensor_count)
     part_here = jnp.dot(rows_here, projection, preferred_element_type=F32).astype(BF16)
     chip_part = (part_here.astype(F32) + part_away.astype(F32)).astype(BF16)
-    chip_part = chip_part.reshape(side_x, chips, TOK_DEV, side_y * part_width)
-    chip_part = jnp.transpose(chip_part, (1, 0, 2, 3))
-    chip_part, pick, combine, residual, norm_gain = lax.optimization_barrier(
-        (chip_part, pick, combine, residual, norm_gain)
-    )
+    chip_part = chip_part.reshape(chips, side_x, TOK_DEV, -1)
+    chip_part, residual, norm_gain = lax.optimization_barrier((chip_part, residual, norm_gain))
     head_parts = along_z(chip_part, same_core)
     sums = jnp.sum(head_parts.astype(F32), axis=0).astype(BF16)
     sums = [sums[0]] + [shift(sums[d], 0, -d, side_y, side_x) for d in range(1, side_x)]
@@ -228,7 +261,7 @@
     )
     rows = arrived.reshape(expert_count * capacity, width)
 
-    result = experts(rows, w_gate[0], w_up[0], w_down[0], gate_other, up_other, down_other)
+    result = experts(rows, gate_own, up_own, down_own, gate_other, up_other, down_other)
     result = result.reshape(expert_count, capacity, width)
     returned = lax.all_to_all(result, "expert", split_axis=0, concat_axis=0, tiled=True)
     expert_part = jnp.dot(combine, returned.reshape(expert_count * capacity, width), preferred_element_type=F32)

time: 247 us -> 239 us (0.968)
  matrix products: 13.9 us -> 3.36 us
  waiting for transfers between devices: 15.5 us -> 19.9 us
  other arithmetic: 6.8 us -> 3.12 us
  Pallas kernels: 10.8 us -> 13.9 us
    sub x1 -> x0, matrix products: 5.02 us -> none  [attend(): weights = jnp.exp(jnp.where(visible, scores - highest, -1e+30))]
    ppermute x9, waiting for transfers between devices: 14.5 us -> 18.1 us  [shift(): return lax.ppermute(array, 'expert', pairs)]
    pallas_call x0 -> x1, Pallas kernels: none -> 3.02 us  [attend(): pl.pallas_call(attend_kernel, grid_spec=pltpu.PrefetchScalarGridSpec(num_...]
    dot_general x1 -> x0, matrix products: 3 us -> none  [attend(): jnp.einsum('hnc,cd->nhd', weights.astype(BF16), value_rows, preferred_ele...]
  transfers between devices with their start and end apart: 13 -> 13, of which waited for: 6 -> 7; matrix products, arithmetic and copies ran while one was open for 5% -> 1% of each run, Pallas kernels for 0% -> 1%
where the time goes in v4:
time: 239 us
  blocking collectives  176 us (74%)
  waiting for transfers between devices  19.9 us (8%)
  starting transfers between devices  17 us (7%)
  Pallas kernels  13.9 us (6%)
  local copies, waits for them, and re-layouts  4.15 us (2%)
  matrix products  3.36 us (1%)
  other arithmetic  3.12 us (1%)
    all_to_all x3, blocking collectives, along_z(): lax.all_to_all(array, 'tensor', split_axis=0, concat_axis=0, tiled=True,...  96.9 us
    all_to_all x1, blocking collectives, shards(): lax.all_to_all(outgoing.reshape(expert_count, capacity, width), 'expert',...  42.3 us
    all_to_all x1, blocking collectives, shards(): lax.all_to_all(result, 'expert', split_axis=0, concat_axis=0, tiled=True)  36.8 us
    ppermute x9, waiting for transfers between devices, shift(): return lax.ppermute(array, 'expert', pairs)  18.1 us
    ppermute x9, starting transfers between devices, shift(): return lax.ppermute(array, 'expert', pairs)  16.2 us
    pallas_call x1, Pallas kernels, experts(): pl.pallas_call(experts_kernel, in_specs=[whole] + [pl.BlockSpec(memory_sp...  10.8 us
  transfers between devices with their start and end apart: 13, of which 7 were waited for; matrix products, arithmetic and copies ran while one was open for 1% of the time, Pallas kernels for 1%

profile of v4, /device:TPU:2, one launch (start us, length us, event | category | flops | bytes accessed | tf_op | source)
XLA Modules:
  0.0 238.6 jit_solution(17618429084022020642)
XLA Ops:
  1.3 3.2 %collective-permute-start.1 = (bf16[512,256]{1,0:T(8,128)(2,1)}, bf16[512,256]{1,0:T(8,128)(2,1)S(1)}, u32[]{:S(2)}, u32[]{:S(2)}) collective-permute-start(bf16[512,256]{1,0:T(8,128)(2,1)} %param.14), channel_id=1, source_target_pairs={{0,128},{16,144},{32,160},{48,176},{64,192},{80,208},{96,224},{112... | collective-permute-start | bytes 786440 | tf_op jit(solution)/shard_map/ppermute | solution.py:33
  5.2 2.6 %collective-permute-start.2 = (bf16[512,256]{1,0:T(8,128)(2,1)}, bf16[512,256]{1,0:T(8,128)(2,1)S(1)}, u32[]{:S(2)}, u32[]{:S(2)}) collective-permute-start(bf16[512,256]{1,0:T(8,128)(2,1)} %param.14), channel_id=1, source_target_pairs={{0,192},{16,208},{32,224},{48,240},{64,0},{80,16},{96,32},{112,48}... | collective-permute-start | bytes 786440 | tf_op jit(solution)/shard_map/ppermute | solution.py:33
  7.7 1.7 copy-done
  9.5 0.9 copy-done.1
  10.4 3.0 %shard_map.109 = bf16[2,8,16,512]{3,2,1,0:T(8,128)(2,1)S(1)} custom-call(s32[3]{0:T(128)S(1)} %pad_add_fusion.scalars, bf16[256,512]{1,0:T(8,128)(2,1)S(1)} %copy-done.1, bf16[1,4,1280,256]{3,2,1,0:T(8,128)(2,1)S(1)} %copy-done), custom_call_target="tpu_custom_call" | custom-call | flops 671088640 | bytes 1179648 | tf_op jit(solution)/shard_map/pallas_call | solution.py:151
  13.5 3.5 %collective-permute-done = bf16[512,256]{1,0:T(8,128)(2,1)S(1)} collective-permute-done((bf16[512,256]{1,0:T(8,128)(2,1)}, bf16[512,256]{1,0:T(8,128)(2,1)S(1)}, u32[]{:S(2)}, u32[]{:S(2)}) %collective-permute-start) | collective-permute-done | bytes 262176 | tf_op jit(solution)/shard_map/ppermute | solution.py:33
  19.4 2.1 collective-permute-start.7
  21.5 1.0 collective-permute-start.6
  22.5 1.8 collective-permute-start.5
  24.6 3.6 %collective-permute-done.7 = bf16[2,8,16,512]{3,2,1,0:T(8,128)(2,1)S(1)} collective-permute-done((bf16[2,8,16,512]{3,2,1,0:T(8,128)(2,1)S(1)}, bf16[2,8,16,512]{3,2,1,0:T(8,128)(2,1)S(1)}, u32[]{:S(2)}, u32[]{:S(2)}) %collective-permute-start.7) | collective-permute-done | bytes 262176 | tf_op jit(solution)/shard_map/ppermute | solution.py:33
  28.2 6.5 %collective-permute-done.6 = bf16[2,8,16,512]{3,2,1,0:T(8,128)(2,1)S(1)} collective-permute-done((bf16[2,8,16,512]{3,2,1,0:T(8,128)(2,1)S(1)}, bf16[2,8,16,512]{3,2,1,0:T(8,128)(2,1)S(1)}, u32[]{:S(2)}, u32[]{:S(2)}) %collective-permute-start.6) | collective-permute-done | bytes 262176 | tf_op jit(solution)/shard_map/ppermute | solution.py:33
  34.6 0.9 collective-permute-done.5
  37.6 1.8 collective-permute-done.9
  39.9 37.4 %all_to_all.25 = bf16[8,4,16,1024]{3,2,1,0:T(8,128)(2,1)S(1)} all-to-all(bf16[8,4,16,1024]{3,2,1,0:T(8,128)(2,1)S(1)} %bitcast.79), channel_id=1, replica_groups={{0,2,4,6,8,10,12,14},{1,3,5,7,9,11,13,15},{16,18,20,22,24,26,28,30},{17..., dimensions={0} | all-to-all | bytes 2097152 | tf_op jit(solution)/shard_map/all_to_all | solution.py:42
  77.5 2.8 %collective-permute-start.12 = (bf16[16,1024]{1,0:T(8,128)(2,1)S(1)}, bf16[16,1024]{1,0:T(8,128)(2,1)S(1)}, u32[]{:S(2)}, u32[]{:S(2)}) collective-permute-start(bf16[16,1024]{1,0:T(8,128)(2,1)S(1)} %get-tuple-element.66), channel_id=1, source_target_pairs={{0,48},{16,0},{32,16},{48,32},{64,112},{80,64},{96,80},{112,96},{1... | collective-permute-start | bytes 98312 | tf_op jit(solution)/shard_map/ppermute | solution.py:33
  80.5 2.0 collective-permute-start.10
  82.4 3.2 %collective-permute-done.11 = bf16[16,1024]{1,0:T(8,128)(2,1)S(1)} collective-permute-done((bf16[16,1024]{1,0:T(8,128)(2,1)S(1)}, bf16[16,1024]{1,0:T(8,128)(2,1)S(1)}, u32[]{:S(2)}, u32[]{:S(2)}) %collective-permute-start.11) | collective-permute-done | bytes 32800 | tf_op jit(solution)/shard_map/ppermute | solution.py:33
  86.6 28.9 %all_to_all.26 = bf16[8,16,4096]{2,1,0:T(8,128)(2,1)S(1)} all-to-all(bf16[8,16,4096]{2,1,0:T(8,128)(2,1)S(1)} %broadcast_in_dim.56), channel_id=1, replica_groups={{0,2,4,6,8,10,12,14},{1,3,5,7,9,11,13,15},{16,18,20,22,24,26,28,30},{17..., dimensions={0} | all-to-all | bytes 2097152 | tf_op jit(solution)/shard_map/all_to_all | solution.py:42
  115.6 1.0 convolution_convert_fusion
  116.6 42.3 %all_to_all.27 = bf16[16,24,4096]{2,1,0:T(8,128)(2,1)S(1)} all-to-all(bf16[16,24,4096]{2,1,0:T(8,128)(2,1)S(1)} %bitcast.77), channel_id=1, replica_groups=mesh['expert'=16,'tensor'=16] {'expert'}, dimensions={0} | all-to-all | bytes 6291456 | tf_op jit(solution)/shard_map/all_to_all | solution.py:259
  158.8 10.8 %shard_map.110 = bf16[384,4096]{1,0:T(8,128)(2,1)S(1)} custom-call(bf16[384,4096]{1,0:T(8,128)(2,1)S(1)} %bitcast.73, bf16[4096,384]{1,0:T(8,128)(2,1)S(1)} %bitcast.76, bf16[4096,384]{1,0:T(8,128)(2,1)} %bitcast.89, bf16[4096,384]{1,0:T(8,128)(2,1)} %collective-permute-done.3.gate_b, bf16[4096,384]{1,0:T(8,128)(2,1)} %collective-permute-done.4.up_b, ...), custom_call_target="tpu_custom_call" | custom-call | flops 7247757312 | bytes 25165824 | tf_op jit(solution)/shard_map/pallas_call | solution.py:96
  169.7 36.8 %all_to_all.28 = bf16[16,24,4096]{2,1,0:T(8,128)(2,1)S(1)} all-to-all(bf16[16,24,4096]{2,1,0:T(8,128)(2,1)S(1)} %bitcast.74), channel_id=1, replica_groups=mesh['expert'=16,'tensor'=16] {'expert'}, dimensions={0} | all-to-all | bytes 6291456 | tf_op jit(solution)/shard_map/all_to_all | solution.py:266
  206.4 0.7 convolution_convert_fusion.1
  207.2 30.6 %all_to_all.29 = bf16[8,16,4096]{2,1,0:T(8,128)(2,1)S(1)} all-to-all(bf16[8,16,4096]{2,1,0:T(8,128)(2,1)S(1)} %bitcast.81), channel_id=1, replica_groups={{0,2,4,6,8,10,12,14},{1,3,5,7,9,11,13,15},{16,18,20,22,24,26,28,30},{17..., dimensions={0} | all-to-all | bytes 2097152 | tf_op jit(solution)/shard_map/all_to_all | solution.py:42
  (77 shorter events, 8.3 us)
Async XLA Ops:
  0.0 17.6 %copy-start.7 = (bf16[256,8]{0,1:T(8,128)(2,1)S(1)}, bf16[256,8]{0,1:T(8,128)(2,1)}, u32[]{:S(2)}) copy-start(bf16[256,8]{0,1:T(8,128)(2,1)} %param.18) | copy-start | bytes 12292
  0.0 17.8 %copy-start.6 = (s32[256,8]{0,1:T(8,128)S(1)}, s32[256,8]{0,1:T(8,128)}, u32[]{:S(2)}) copy-start(s32[256,8]{0,1:T(8,128)} %param.17) | copy-start | bytes 24580
  0.8 16.6 %collective-permute-start.3 = (bf16[4096,384]{1,0:T(8,128)(2,1)}, bf16[4096,384]{1,0:T(8,128)(2,1)}, u32[]{:S(2)}, u32[]{:S(2)}) collective-permute-start(bf16[4096,384]{1,0:T(8,128)(2,1)} %bitcast.75), channel_id=1, source_target_pairs={{0,1},{1,0},{2,3},{3,2},{4,5},{5,4},{6,7},{7,6},{8,9},{9,8},{10,11... | collective-permute-start | bytes 9437192 | tf_op jit(solution)/shard_map/ppermute | solution.py:24
  0.8 16.5 %collective-permute-start.4 = (bf16[4096,384]{1,0:T(8,128)(2,1)}, bf16[4096,384]{1,0:T(8,128)(2,1)}, u32[]{:S(2)}, u32[]{:S(2)}) collective-permute-start(bf16[4096,384]{1,0:T(8,128)(2,1)} %bitcast.88), channel_id=1, source_target_pairs={{0,1},{1,0},{2,3},{3,2},{4,5},{5,4},{6,7},{7,6},{8,9},{9,8},{10,11... | collective-permute-start | bytes 9437192 | tf_op jit(solution)/shard_map/ppermute | solution.py:24
  1.3 12.2 %collective-permute-start.1 = (bf16[512,256]{1,0:T(8,128)(2,1)}, bf16[512,256]{1,0:T(8,128)(2,1)S(1)}, u32[]{:S(2)}, u32[]{:S(2)}) collective-permute-start(bf16[512,256]{1,0:T(8,128)(2,1)} %param.14), channel_id=1, source_target_pairs={{0,128},{16,144},{32,160},{48,176},{64,192},{80,208},{96,224},{112... | collective-permute-start | bytes 786440 | tf_op jit(solution)/shard_map/ppermute | solution.py:33
  4.5 12.5 %collective-permute-start = (bf16[512,256]{1,0:T(8,128)(2,1)}, bf16[512,256]{1,0:T(8,128)(2,1)S(1)}, u32[]{:S(2)}, u32[]{:S(2)}) collective-permute-start(bf16[512,256]{1,0:T(8,128)(2,1)} %param.14), channel_id=1, source_target_pairs={{0,64},{16,80},{32,96},{48,112},{64,128},{80,144},{96,160},{112,17... | collective-permute-start | bytes 786440 | tf_op jit(solution)/shard_map/ppermute | solution.py:33
  5.2 12.2 %collective-permute-start.2 = (bf16[512,256]{1,0:T(8,128)(2,1)}, bf16[512,256]{1,0:T(8,128)(2,1)S(1)}, u32[]{:S(2)}, u32[]{:S(2)}) collective-permute-start(bf16[512,256]{1,0:T(8,128)(2,1)} %param.14), channel_id=1, source_target_pairs={{0,192},{16,208},{32,224},{48,240},{64,0},{80,16},{96,32},{112,48}... | collective-permute-start | bytes 786440 | tf_op jit(solution)/shard_map/ppermute | solution.py:33
  7.7 1.7 copy-start
  9.5 0.9 copy-start.1
  10.4 13.9 %copy-start.3 = (bf16[512,256]{1,0:T(8,128)(2,1)S(1)}, bf16[512,256]{1,0:T(8,128)(2,1)}, u32[]{:S(2)}) copy-start(bf16[512,256]{1,0:T(8,128)(2,1)} %param.14) | copy-start | bytes 786436
  17.3 18.2 %collective-permute-start.8 = (bf16[384,4096]{1,0:T(8,128)(2,1)}, bf16[384,4096]{1,0:T(8,128)(2,1)}, u32[]{:S(2)}, u32[]{:S(2)}) collective-permute-start(bf16[384,4096]{1,0:T(8,128)(2,1)} %bitcast.90), channel_id=1, source_target_pairs={{0,1},{1,0},{2,3},{3,2},{4,5},{5,4},{6,7},{7,6},{8,9},{9,8},{10,11... | collective-permute-start | bytes 9437192 | tf_op jit(solution)/shard_map/ppermute | solution.py:24
  19.4 8.7 %collective-permute-start.7 = (bf16[2,8,16,512]{3,2,1,0:T(8,128)(2,1)S(1)}, bf16[2,8,16,512]{3,2,1,0:T(8,128)(2,1)S(1)}, u32[]{:S(2)}, u32[]{:S(2)}) collective-permute-start(bf16[2,8,16,512]{3,2,1,0:T(8,128)(2,1)S(1)} %shard_map.109), channel_id=1, source_target_pairs={{0,48},{16,0},{32,16},{48,32},{64,112},{80,64},{96,80},{112,96},{1... | collective-permute-start | bytes 786440 | tf_op jit(solution)/shard_map/ppermute | solution.py:33
  21.5 13.1 %collective-permute-start.6 = (bf16[2,8,16,512]{3,2,1,0:T(8,128)(2,1)S(1)}, bf16[2,8,16,512]{3,2,1,0:T(8,128)(2,1)S(1)}, u32[]{:S(2)}, u32[]{:S(2)}) collective-permute-start(bf16[2,8,16,512]{3,2,1,0:T(8,128)(2,1)S(1)} %shard_map.109), channel_id=1, source_target_pairs={{0,32},{16,48},{32,0},{48,16},{64,96},{80,112},{96,64},{112,80},{1... | collective-permute-start | bytes 786440 | tf_op jit(solution)/shard_map/ppermute | solution.py:33
  22.5 13.1 %collective-permute-start.5 = (bf16[2,8,16,512]{3,2,1,0:T(8,128)(2,1)S(1)}, bf16[2,8,16,512]{3,2,1,0:T(8,128)(2,1)S(1)}, u32[]{:S(2)}, u32[]{:S(2)}) collective-permute-start(bf16[2,8,16,512]{3,2,1,0:T(8,128)(2,1)S(1)} %shard_map.109), channel_id=1, source_target_pairs={{0,16},{16,32},{32,48},{48,0},{64,80},{80,96},{96,112},{112,64},{1... | collective-permute-start | bytes 786440 | tf_op jit(solution)/shard_map/ppermute | solution.py:33
  36.5 2.9 %collective-permute-start.9 = (bf16[512,1024]{1,0:T(8,128)(2,1)S(1)}, bf16[512,1024]{1,0:T(8,128)(2,1)S(1)}, u32[]{:S(2)}, u32[]{:S(2)}) collective-permute-start(bf16[512,1024]{1,0:T(8,128)(2,1)S(1)} %convolution_convert_fusion.2), channel_id=1, source_target_pairs={{0,1},{1,0},{2,3},{3,2},{4,5},{5,4},{6,7},{7,6},{8,9},{9,8},{10,11... | collective-permute-start | bytes 3145736 | tf_op jit(solution)/shard_map/ppermute | solution.py:24
  39.8 46.4 %copy-start.4 = (bf16[16,4096]{1,0:T(8,128)(2,1)S(1)}, bf16[16,4096]{1,0:T(8,128)(2,1)}, u32[]{:S(2)}) copy-start(bf16[16,4096]{1,0:T(8,128)(2,1)} %param.15) | copy-start | bytes 393220
  39.9 46.6 %copy-start.5 = (f32[4096]{0:T(1024)S(1)}, f32[4096]{0:T(1024)}, u32[]{:S(2)}) copy-start(f32[4096]{0:T(1024)} %param.16) | copy-start | bytes 49156
  77.5 4.9 %collective-permute-start.12 = (bf16[16,1024]{1,0:T(8,128)(2,1)S(1)}, bf16[16,1024]{1,0:T(8,128)(2,1)S(1)}, u32[]{:S(2)}, u32[]{:S(2)}) collective-permute-start(bf16[16,1024]{1,0:T(8,128)(2,1)S(1)} %get-tuple-element.66), channel_id=1, source_target_pairs={{0,48},{16,0},{32,16},{48,32},{64,112},{80,64},{96,80},{112,96},{1... | collective-permute-start | bytes 98312 | tf_op jit(solution)/shard_map/ppermute | solution.py:33
  80.3 5.4 %collective-permute-start.11 = (bf16[16,1024]{1,0:T(8,128)(2,1)S(1)}, bf16[16,1024]{1,0:T(8,128)(2,1)S(1)}, u32[]{:S(2)}, u32[]{:S(2)}) collective-permute-start(bf16[16,1024]{1,0:T(8,128)(2,1)S(1)} %get-tuple-element.67), channel_id=1, source_target_pairs={{0,32},{16,48},{32,0},{48,16},{64,96},{80,112},{96,64},{112,80},{1... | collective-permute-start | bytes 98312 | tf_op jit(solution)/shard_map/ppermute | solution.py:33
  80.5 5.3 %collective-permute-start.10 = (bf16[16,1024]{1,0:T(8,128)(2,1)S(1)}, bf16[16,1024]{1,0:T(8,128)(2,1)S(1)}, u32[]{:S(2)}, u32[]{:S(2)}) collective-permute-start(bf16[16,1024]{1,0:T(8,128)(2,1)S(1)} %get-tuple-element.68), channel_id=1, source_target_pairs={{0,16},{16,32},{32,48},{48,0},{64,80},{80,96},{96,112},{112,64},{1... | collective-permute-start | bytes 98312 | tf_op jit(solution)/shard_map/ppermute | solution.py:33
  116.5 42.3 %copy-start.2 = (bf16[1,4096,384]{2,1,0:T(8,128)(2,1)S(1)}, bf16[1,4096,384]{2,1,0:T(8,128)(2,1)}, u32[]{:S(2)}) copy-start(bf16[1,4096,384]{2,1,0:T(8,128)(2,1)} %param.19) | copy-start | bytes 9437188

commit v5 on v4

--- a/solution.py
+++ b/solution.py
@@ -223,16 +223,16 @@
     scalars = jnp.stack([kv_index, prefix_len[0], core]).astype(jnp.int32)
     scalars, gate_own, up_own, down_own = lax.optimization_barrier((scalars, w_gate[0], w_up[0], w_down[0]))
     gate_other = chip_swap(gate_own, tensor_count)
+    attended = attend(scalars, queries, keys_values)
+    attended, blocks, gate_other, up_own, down_own, pick = lax.optimization_barrier(
+        (attended, blocks, gate_other, up_own, down_own, pick)
+    )
     up_other = chip_swap(up_own, tensor_count)
-    attended = attend(scalars, queries, keys_values)
-    attended, blocks, gate_other, up_other, down_own = lax.optimization_barrier(
-        (attended, blocks, gate_other, up_other, down_own)
-    )
     down_other = chip_swap(down_own, tensor_count)
     projection = jnp.concatenate(ordered(blocks, place_y), axis=1)
     pieces = [attended] + [shift(attended, 0, d, side_y, side_x) for d in range(1, side_x)]
-    pieces, projection, pick, combine, down_other = lax.optimization_barrier(
-        (pieces, projection, pick, combine, down_other)
+    pieces, projection, combine, up_other, down_other = lax.optimization_barrier(
+        (pieces, projection, combine, up_other, down_other)
     )
     rows_away = jnp.stack([piece[0] for piece in pieces], axis=1).reshape(-1, per_device * HD)
     rows_here = jnp.stack([piece[1] for piece in pieces], axis=1).reshape(-1, per_device * HD)

time: 239 us -> 238 us (level)
  transfers between devices with their start and end apart: 13 -> 13, of which waited for: 7 -> 7; matrix products, arithmetic and copies ran while one was open for 1% -> 2% of each run, Pallas kernels for 1% -> 1%
where the time goes in v5:
time: 238 us; the launch traced here: 237 us
  blocking collectives  176 us (74%)
  waiting for transfers between devices  18 us (8%)
  starting transfers between devices  17.1 us (7%)
  Pallas kernels  13.9 us (6%)
  local copies, waits for them, and re-layouts  4.83 us (2%)
  matrix products  3.36 us (1%)
  other arithmetic  3.14 us (1%)
    all_to_all x3, blocking collectives, along_z(): lax.all_to_all(array, 'tensor', split_axis=0, concat_axis=0, tiled=True,...  96.9 us
    all_to_all x1, blocking collectives, shards(): lax.all_to_all(outgoing.reshape(expert_count, capacity, width), 'expert',...  42.3 us
    all_to_all x1, blocking collectives, shards(): lax.all_to_all(result, 'expert', split_axis=0, concat_axis=0, tiled=True)  36.8 us
    ppermute x9, starting transfers between devices, shift(): return lax.ppermute(array, 'expert', pairs)  16.3 us
    ppermute x9, waiting for transfers between devices, shift(): return lax.ppermute(array, 'expert', pairs)  16.2 us
    pallas_call x1, Pallas kernels, experts(): pl.pallas_call(experts_kernel, in_specs=[whole] + [pl.BlockSpec(memory_sp...  10.8 us
  transfers between devices with their start and end apart: 13, of which 7 were waited for; matrix products, arithmetic and copies ran while one was open for 2% of the time, Pallas kernels for 1%

profile of v5, /device:TPU:2, one launch (start us, length us, event | category | flops | bytes accessed | tf_op | source)
XLA Modules:
  0.0 237.4 jit_solution(15224118746207363090)
XLA Ops:
  0.8 3.3 %collective-permute-start.1 = (bf16[512,256]{1,0:T(8,128)(2,1)}, bf16[512,256]{1,0:T(8,128)(2,1)S(1)}, u32[]{:S(2)}, u32[]{:S(2)}) collective-permute-start(bf16[512,256]{1,0:T(8,128)(2,1)} %param.14), channel_id=1, source_target_pairs={{0,128},{16,144},{32,160},{48,176},{64,192},{80,208},{96,224},{112... | collective-permute-start | bytes 786440 | tf_op jit(solution)/shard_map/ppermute | solution.py:33
  4.8 2.6 %collective-permute-start.2 = (bf16[512,256]{1,0:T(8,128)(2,1)}, bf16[512,256]{1,0:T(8,128)(2,1)S(1)}, u32[]{:S(2)}, u32[]{:S(2)}) collective-permute-start(bf16[512,256]{1,0:T(8,128)(2,1)} %param.14), channel_id=1, source_target_pairs={{0,192},{16,208},{32,224},{48,240},{64,0},{80,16},{96,32},{112,48}... | collective-permute-start | bytes 786440 | tf_op jit(solution)/shard_map/ppermute | solution.py:33
  7.5 0.8 reshape.242
  9.2 1.7 copy-done
  11.0 0.9 copy-done.1
  11.9 3.1 %shard_map.109 = bf16[2,8,16,512]{3,2,1,0:T(8,128)(2,1)S(1)} custom-call(s32[3]{0:T(128)S(1)} %pad_add_fusion.scalars, bf16[256,512]{1,0:T(8,128)(2,1)S(1)} %copy-done.1, bf16[1,4,1280,256]{3,2,1,0:T(8,128)(2,1)S(1)} %copy-done), custom_call_target="tpu_custom_call" | custom-call | flops 671088640 | bytes 1179648 | tf_op jit(solution)/shard_map/pallas_call | solution.py:151
  15.0 1.9 collective-permute-done
  18.6 2.0 collective-permute-start.6
  20.6 1.1 collective-permute-start.5
  21.6 1.8 collective-permute-start.4
  23.7 3.5 %collective-permute-done.6 = bf16[2,8,16,512]{3,2,1,0:T(8,128)(2,1)S(1)} collective-permute-done((bf16[2,8,16,512]{3,2,1,0:T(8,128)(2,1)S(1)}, bf16[2,8,16,512]{3,2,1,0:T(8,128)(2,1)S(1)}, u32[]{:S(2)}, u32[]{:S(2)}) %collective-permute-start.6) | collective-permute-done | bytes 262176 | tf_op jit(solution)/shard_map/ppermute | solution.py:33
  27.3 6.2 %collective-permute-done.5 = bf16[2,8,16,512]{3,2,1,0:T(8,128)(2,1)S(1)} collective-permute-done((bf16[2,8,16,512]{3,2,1,0:T(8,128)(2,1)S(1)}, bf16[2,8,16,512]{3,2,1,0:T(8,128)(2,1)S(1)}, u32[]{:S(2)}, u32[]{:S(2)}) %collective-permute-start.5) | collective-permute-done | bytes 262176 | tf_op jit(solution)/shard_map/ppermute | solution.py:33
  33.4 0.9 collective-permute-done.4
  36.4 1.8 collective-permute-done.9
  38.7 37.4 %all_to_all.25 = bf16[8,4,16,1024]{3,2,1,0:T(8,128)(2,1)S(1)} all-to-all(bf16[8,4,16,1024]{3,2,1,0:T(8,128)(2,1)S(1)} %bitcast.79), channel_id=1, replica_groups={{0,2,4,6,8,10,12,14},{1,3,5,7,9,11,13,15},{16,18,20,22,24,26,28,30},{17..., dimensions={0} | all-to-all | bytes 2097152 | tf_op jit(solution)/shard_map/all_to_all | solution.py:42
  76.3 2.8 %collective-permute-start.12 = (bf16[16,1024]{1,0:T(8,128)(2,1)S(1)}, bf16[16,1024]{1,0:T(8,128)(2,1)S(1)}, u32[]{:S(2)}, u32[]{:S(2)}) collective-permute-start(bf16[16,1024]{1,0:T(8,128)(2,1)S(1)} %get-tuple-element.68), channel_id=1, source_target_pairs={{0,48},{16,0},{32,16},{48,32},{64,112},{80,64},{96,80},{112,96},{1... | collective-permute-start | bytes 98312 | tf_op jit(solution)/shard_map/ppermute | solution.py:33
  79.3 2.0 collective-permute-start.10
  81.2 3.2 %collective-permute-done.11 = bf16[16,1024]{1,0:T(8,128)(2,1)S(1)} collective-permute-done((bf16[16,1024]{1,0:T(8,128)(2,1)S(1)}, bf16[16,1024]{1,0:T(8,128)(2,1)S(1)}, u32[]{:S(2)}, u32[]{:S(2)}) %collective-permute-start.11) | collective-permute-done | bytes 32800 | tf_op jit(solution)/shard_map/ppermute | solution.py:33
  85.4 28.9 %all_to_all.26 = bf16[8,16,4096]{2,1,0:T(8,128)(2,1)S(1)} all-to-all(bf16[8,16,4096]{2,1,0:T(8,128)(2,1)S(1)} %broadcast_in_dim.56), channel_id=1, replica_groups={{0,2,4,6,8,10,12,14},{1,3,5,7,9,11,13,15},{16,18,20,22,24,26,28,30},{17..., dimensions={0} | all-to-all | bytes 2097152 | tf_op jit(solution)/shard_map/all_to_all | solution.py:42
  114.4 1.0 convolution_convert_fusion
  115.4 42.3 %all_to_all.27 = bf16[16,24,4096]{2,1,0:T(8,128)(2,1)S(1)} all-to-all(bf16[16,24,4096]{2,1,0:T(8,128)(2,1)S(1)} %bitcast.77), channel_id=1, replica_groups=mesh['expert'=16,'tensor'=16] {'expert'}, dimensions={0} | all-to-all | bytes 6291456 | tf_op jit(solution)/shard_map/all_to_all | solution.py:259
  157.6 10.8 %shard_map.110 = bf16[384,4096]{1,0:T(8,128)(2,1)S(1)} custom-call(bf16[384,4096]{1,0:T(8,128)(2,1)S(1)} %bitcast.73, bf16[4096,384]{1,0:T(8,128)(2,1)S(1)} %bitcast.76, bf16[4096,384]{1,0:T(8,128)(2,1)} %bitcast.3.up_a, bf16[4096,384]{1,0:T(8,128)(2,1)} %collective-permute-done.3.gate_b, bf16[4096,384]{1,0:T(8,128)(2,1)} %collective-permute-done.7.up_b, ...), custom_call_target="tpu_custom_call" | custom-call | flops 7247757312 | bytes 25165824 | tf_op jit(solution)/shard_map/pallas_call | solution.py:96
  168.5 36.8 %all_to_all.28 = bf16[16,24,4096]{2,1,0:T(8,128)(2,1)S(1)} all-to-all(bf16[16,24,4096]{2,1,0:T(8,128)(2,1)S(1)} %bitcast.74), channel_id=1, replica_groups=mesh['expert'=16,'tensor'=16] {'expert'}, dimensions={0} | all-to-all | bytes 6291456 | tf_op jit(solution)/shard_map/all_to_all | solution.py:266
  206.0 30.6 %all_to_all.29 = bf16[8,16,4096]{2,1,0:T(8,128)(2,1)S(1)} all-to-all(bf16[8,16,4096]{2,1,0:T(8,128)(2,1)S(1)} %bitcast.81), channel_id=1, replica_groups={{0,2,4,6,8,10,12,14},{1,3,5,7,9,11,13,15},{16,18,20,22,24,26,28,30},{17..., dimensions={0} | all-to-all | bytes 2097152 | tf_op jit(solution)/shard_map/all_to_all | solution.py:42
  (75 shorter events, 8.9 us)
Async XLA Ops:
  0.0 23.4 %copy-start.3 = (bf16[512,256]{1,0:T(8,128)(2,1)S(1)}, bf16[512,256]{1,0:T(8,128)(2,1)}, u32[]{:S(2)}) copy-start(bf16[512,256]{1,0:T(8,128)(2,1)} %param.14) | copy-start | bytes 786436
  0.0 17.8 %copy-start.6 = (bf16[256,8]{0,1:T(8,128)(2,1)S(1)}, bf16[256,8]{0,1:T(8,128)(2,1)}, u32[]{:S(2)}) copy-start(bf16[256,8]{0,1:T(8,128)(2,1)} %param.18) | copy-start | bytes 12292
  0.8 16.5 %collective-permute-start.3 = (bf16[4096,384]{1,0:T(8,128)(2,1)}, bf16[4096,384]{1,0:T(8,128)(2,1)}, u32[]{:S(2)}, u32[]{:S(2)}) collective-permute-start(bf16[4096,384]{1,0:T(8,128)(2,1)} %bitcast.75), channel_id=1, source_target_pairs={{0,1},{1,0},{2,3},{3,2},{4,5},{5,4},{6,7},{7,6},{8,9},{9,8},{10,11... | collective-permute-start | bytes 9437192 | tf_op jit(solution)/shard_map/ppermute | solution.py:24
  0.8 14.2 %collective-permute-start.1 = (bf16[512,256]{1,0:T(8,128)(2,1)}, bf16[512,256]{1,0:T(8,128)(2,1)S(1)}, u32[]{:S(2)}, u32[]{:S(2)}) collective-permute-start(bf16[512,256]{1,0:T(8,128)(2,1)} %param.14), channel_id=1, source_target_pairs={{0,128},{16,144},{32,160},{48,176},{64,192},{80,208},{96,224},{112... | collective-permute-start | bytes 786440 | tf_op jit(solution)/shard_map/ppermute | solution.py:33
  4.1 12.8 %collective-permute-start = (bf16[512,256]{1,0:T(8,128)(2,1)}, bf16[512,256]{1,0:T(8,128)(2,1)S(1)}, u32[]{:S(2)}, u32[]{:S(2)}) collective-permute-start(bf16[512,256]{1,0:T(8,128)(2,1)} %param.14), channel_id=1, source_target_pairs={{0,64},{16,80},{32,96},{48,112},{64,128},{80,144},{96,160},{112,17... | collective-permute-start | bytes 786440 | tf_op jit(solution)/shard_map/ppermute | solution.py:33
  4.8 12.5 %collective-permute-start.2 = (bf16[512,256]{1,0:T(8,128)(2,1)}, bf16[512,256]{1,0:T(8,128)(2,1)S(1)}, u32[]{:S(2)}, u32[]{:S(2)}) collective-permute-start(bf16[512,256]{1,0:T(8,128)(2,1)} %param.14), channel_id=1, source_target_pairs={{0,192},{16,208},{32,224},{48,240},{64,0},{80,16},{96,32},{112,48}... | collective-permute-start | bytes 786440 | tf_op jit(solution)/shard_map/ppermute | solution.py:33
  9.2 1.7 copy-start
  10.9 0.9 copy-start.1
  17.3 17.1 %collective-permute-start.7 = (bf16[4096,384]{1,0:T(8,128)(2,1)}, bf16[4096,384]{1,0:T(8,128)(2,1)}, u32[]{:S(2)}, u32[]{:S(2)}) collective-permute-start(bf16[4096,384]{1,0:T(8,128)(2,1)} %bitcast.3.up_a), channel_id=1, source_target_pairs={{0,1},{1,0},{2,3},{3,2},{4,5},{5,4},{6,7},{7,6},{8,9},{9,8},{10,11... | collective-permute-start | bytes 9437192 | tf_op jit(solution)/shard_map/ppermute | solution.py:24
  17.3 17.1 %collective-permute-start.8 = (bf16[384,4096]{1,0:T(8,128)(2,1)}, bf16[384,4096]{1,0:T(8,128)(2,1)}, u32[]{:S(2)}, u32[]{:S(2)}) collective-permute-start(bf16[384,4096]{1,0:T(8,128)(2,1)} %bitcast.4.down_a), channel_id=1, source_target_pairs={{0,1},{1,0},{2,3},{3,2},{4,5},{5,4},{6,7},{7,6},{8,9},{9,8},{10,11... | collective-permute-start | bytes 9437192 | tf_op jit(solution)/shard_map/ppermute | solution.py:24
  18.6 8.6 %collective-permute-start.6 = (bf16[2,8,16,512]{3,2,1,0:T(8,128)(2,1)S(1)}, bf16[2,8,16,512]{3,2,1,0:T(8,128)(2,1)S(1)}, u32[]{:S(2)}, u32[]{:S(2)}) collective-permute-start(bf16[2,8,16,512]{3,2,1,0:T(8,128)(2,1)S(1)} %shard_map.109), channel_id=1, source_target_pairs={{0,48},{16,0},{32,16},{48,32},{64,112},{80,64},{96,80},{112,96},{1... | collective-permute-start | bytes 786440 | tf_op jit(solution)/shard_map/ppermute | solution.py:33
  20.6 12.9 %collective-permute-start.5 = (bf16[2,8,16,512]{3,2,1,0:T(8,128)(2,1)S(1)}, bf16[2,8,16,512]{3,2,1,0:T(8,128)(2,1)S(1)}, u32[]{:S(2)}, u32[]{:S(2)}) collective-permute-start(bf16[2,8,16,512]{3,2,1,0:T(8,128)(2,1)S(1)} %shard_map.109), channel_id=1, source_target_pairs={{0,32},{16,48},{32,0},{48,16},{64,96},{80,112},{96,64},{112,80},{1... | collective-permute-start | bytes 786440 | tf_op jit(solution)/shard_map/ppermute | solution.py:33
  21.6 12.7 %collective-permute-start.4 = (bf16[2,8,16,512]{3,2,1,0:T(8,128)(2,1)S(1)}, bf16[2,8,16,512]{3,2,1,0:T(8,128)(2,1)S(1)}, u32[]{:S(2)}, u32[]{:S(2)}) collective-permute-start(bf16[2,8,16,512]{3,2,1,0:T(8,128)(2,1)S(1)} %shard_map.109), channel_id=1, source_target_pairs={{0,16},{16,32},{32,48},{48,0},{64,80},{80,96},{96,112},{112,64},{1... | collective-permute-start | bytes 786440 | tf_op jit(solution)/shard_map/ppermute | solution.py:33
  35.3 2.9 %collective-permute-start.9 = (bf16[512,1024]{1,0:T(8,128)(2,1)S(1)}, bf16[512,1024]{1,0:T(8,128)(2,1)S(1)}, u32[]{:S(2)}, u32[]{:S(2)}) collective-permute-start(bf16[512,1024]{1,0:T(8,128)(2,1)S(1)} %convolution_convert_fusion.2), channel_id=1, source_target_pairs={{0,1},{1,0},{2,3},{3,2},{4,5},{5,4},{6,7},{7,6},{8,9},{9,8},{10,11... | collective-permute-start | bytes 3145736 | tf_op jit(solution)/shard_map/ppermute | solution.py:24
  38.6 46.4 %copy-start.4 = (bf16[16,4096]{1,0:T(8,128)(2,1)S(1)}, bf16[16,4096]{1,0:T(8,128)(2,1)}, u32[]{:S(2)}) copy-start(bf16[16,4096]{1,0:T(8,128)(2,1)} %param.15) | copy-start | bytes 393220
  38.6 46.6 %copy-start.5 = (f32[4096]{0:T(1024)S(1)}, f32[4096]{0:T(1024)}, u32[]{:S(2)}) copy-start(f32[4096]{0:T(1024)} %param.16) | copy-start | bytes 49156
  76.3 4.9 %collective-permute-start.12 = (bf16[16,1024]{1,0:T(8,128)(2,1)S(1)}, bf16[16,1024]{1,0:T(8,128)(2,1)S(1)}, u32[]{:S(2)}, u32[]{:S(2)}) collective-permute-start(bf16[16,1024]{1,0:T(8,128)(2,1)S(1)} %get-tuple-element.68), channel_id=1, source_target_pairs={{0,48},{16,0},{32,16},{48,32},{64,112},{80,64},{96,80},{112,96},{1... | collective-permute-start | bytes 98312 | tf_op jit(solution)/shard_map/ppermute | solution.py:33
  79.1 5.4 %collective-permute-start.11 = (bf16[16,1024]{1,0:T(8,128)(2,1)S(1)}, bf16[16,1024]{1,0:T(8,128)(2,1)S(1)}, u32[]{:S(2)}, u32[]{:S(2)}) collective-permute-start(bf16[16,1024]{1,0:T(8,128)(2,1)S(1)} %get-tuple-element.69), channel_id=1, source_target_pairs={{0,32},{16,48},{32,0},{48,16},{64,96},{80,112},{96,64},{112,80},{1... | collective-permute-start | bytes 98312 | tf_op jit(solution)/shard_map/ppermute | solution.py:33
  79.3 5.3 %collective-permute-start.10 = (bf16[16,1024]{1,0:T(8,128)(2,1)S(1)}, bf16[16,1024]{1,0:T(8,128)(2,1)S(1)}, u32[]{:S(2)}, u32[]{:S(2)}) collective-permute-start(bf16[16,1024]{1,0:T(8,128)(2,1)S(1)} %get-tuple-element.70), channel_id=1, source_target_pairs={{0,16},{16,32},{32,48},{48,0},{64,80},{80,96},{96,112},{112,64},{1... | collective-permute-start | bytes 98312 | tf_op jit(solution)/shard_map/ppermute | solution.py:33
  115.3 42.3 %copy-start.2 = (bf16[1,4096,384]{2,1,0:T(8,128)(2,1)S(1)}, bf16[1,4096,384]{2,1,0:T(8,128)(2,1)}, u32[]{:S(2)}) copy-start(bf16[1,4096,384]{2,1,0:T(8,128)(2,1)} %param.19) | copy-start | bytes 9437188

commit v6 on v5

--- a/solution.py
+++ b/solution.py
@@ -51,7 +51,7 @@
     chunk = depth // steps
 
     def wide_copy(step, place):
-        span = pl.ds(pl.multiple_of(step * chunk, chunk), chunk)
+        span = pl.ds(step * chunk, chunk)
         source = (gate_a, gate_b, up_a, up_b)[place]
         target = wide.at[span, pl.ds(place * hidden, hidden)]
         return pltpu.make_async_copy(source.at[span, :], target, wide_sems.at[step, place])
@@ -65,16 +65,16 @@
             wide_copy(step, place).start()
     for place in range(2):
         tall_copy(place).start()
-    total[...] = jnp.zeros_like(total)
-
-    def multiply(step, carry):
+
+    def multiply(step, first):
         for place in range(4):
             wide_copy(step, place).wait()
-        span = pl.ds(pl.multiple_of(step * chunk, chunk), chunk)
-        total[...] += jnp.dot(rows[:, span], wide[span, :], preferred_element_type=F32)
-        return carry
-
-    lax.fori_loop(0, steps, multiply, 0)
+        span = pl.ds(step * chunk, chunk)
+        term = jnp.dot(rows[:, span], wide[span, :], preferred_element_type=F32)
+        total[...] = term if first else total[...] + term
+
+    for step in range(steps):
+        multiply(step, step == 0)
     value = total[:, : 2 * hidden]
     inner[...] = (value / (1.0 + jnp.exp(-value)) * total[:, 2 * hidden :]).astype(BF16)
     for place in range(2):
@@ -91,7 +91,7 @@
 def experts(rows, gate_a, up_a, down_a, gate_b, up_b, down_b):
     count, depth = rows.shape
     hidden = gate_a.shape[1]
-    steps = 4
+    steps = 2
     whole = pl.BlockSpec(memory_space=pltpu.VMEM)
     return pl.pallas_call(
         experts_kernel,

time: 238 us -> 237 us (level)
  no operation moved by 1% of the time
where the time goes in v6:
time: 237 us
  blocking collectives  176 us (74%)
  waiting for transfers between devices  18 us (8%)
  starting transfers between devices  17.1 us (7%)
  Pallas kernels  13.6 us (6%)
  local copies, waits for them, and re-layouts  4.83 us (2%)
  matrix products  3.36 us (1%)
  other arithmetic  3.14 us (1%)
    all_to_all x3, blocking collectives, along_z(): lax.all_to_all(array, 'tensor', split_axis=0, concat_axis=0, tiled=True,...  96.9 us
    all_to_all x1, blocking collectives, shards(): lax.all_to_all(outgoing.reshape(expert_count, capacity, width), 'expert',...  42.3 us
    all_to_all x1, blocking collectives, shards(): lax.all_to_all(result, 'expert', split_axis=0, concat_axis=0, tiled=True)  36.8 us
    ppermute x9, starting transfers between devices, shift(): return lax.ppermute(array, 'expert', pairs)  16.3 us
    ppermute x9, waiting for transfers between devices, shift(): return lax.ppermute(array, 'expert', pairs)  16.2 us
    pallas_call x1, Pallas kernels, experts(): pl.pallas_call(experts_kernel, in_specs=[whole] + [pl.BlockSpec(memory_sp...  10.5 us
  transfers between devices with their start and end apart: 13, of which 7 were waited for; matrix products, arithmetic and copies ran while one was open for 2% of the time, Pallas kernels for 1%

profile of v6, /device:TPU:2, one launch (start us, length us, event | category | flops | bytes accessed | tf_op | source)
XLA Modules:
  0.0 237.0 jit_solution(8023641795542021227)
XLA Ops:
  0.8 3.3 %collective-permute-start.1 = (bf16[512,256]{1,0:T(8,128)(2,1)}, bf16[512,256]{1,0:T(8,128)(2,1)S(1)}, u32[]{:S(2)}, u32[]{:S(2)}) collective-permute-start(bf16[512,256]{1,0:T(8,128)(2,1)} %param.14), channel_id=1, source_target_pairs={{0,128},{16,144},{32,160},{48,176},{64,192},{80,208},{96,224},{112... | collective-permute-start | bytes 786440 | tf_op jit(solution)/shard_map/ppermute | solution.py:33
  4.8 2.6 %collective-permute-start.2 = (bf16[512,256]{1,0:T(8,128)(2,1)}, bf16[512,256]{1,0:T(8,128)(2,1)S(1)}, u32[]{:S(2)}, u32[]{:S(2)}) collective-permute-start(bf16[512,256]{1,0:T(8,128)(2,1)} %param.14), channel_id=1, source_target_pairs={{0,192},{16,208},{32,224},{48,240},{64,0},{80,16},{96,32},{112,48}... | collective-permute-start | bytes 786440 | tf_op jit(solution)/shard_map/ppermute | solution.py:33
  7.5 0.8 reshape.242
  9.2 1.7 copy-done
  11.0 0.9 copy-done.1
  11.9 3.1 %shard_map.109 = bf16[2,8,16,512]{3,2,1,0:T(8,128)(2,1)S(1)} custom-call(s32[3]{0:T(128)S(1)} %pad_add_fusion.scalars, bf16[256,512]{1,0:T(8,128)(2,1)S(1)} %copy-done.1, bf16[1,4,1280,256]{3,2,1,0:T(8,128)(2,1)S(1)} %copy-done), custom_call_target="tpu_custom_call" | custom-call | flops 671088640 | bytes 1179648 | tf_op jit(solution)/shard_map/pallas_call | solution.py:151
  15.0 1.9 collective-permute-done
  18.6 2.0 collective-permute-start.6
  20.6 1.1 collective-permute-start.5
  21.6 1.8 collective-permute-start.4
  23.7 3.5 %collective-permute-done.6 = bf16[2,8,16,512]{3,2,1,0:T(8,128)(2,1)S(1)} collective-permute-done((bf16[2,8,16,512]{3,2,1,0:T(8,128)(2,1)S(1)}, bf16[2,8,16,512]{3,2,1,0:T(8,128)(2,1)S(1)}, u32[]{:S(2)}, u32[]{:S(2)}) %collective-permute-start.6) | collective-permute-done | bytes 262176 | tf_op jit(solution)/shard_map/ppermute | solution.py:33
  27.3 6.2 %collective-permute-done.5 = bf16[2,8,16,512]{3,2,1,0:T(8,128)(2,1)S(1)} collective-permute-done((bf16[2,8,16,512]{3,2,1,0:T(8,128)(2,1)S(1)}, bf16[2,8,16,512]{3,2,1,0:T(8,128)(2,1)S(1)}, u32[]{:S(2)}, u32[]{:S(2)}) %collective-permute-start.5) | collective-permute-done | bytes 262176 | tf_op jit(solution)/shard_map/ppermute | solution.py:33
  33.4 0.9 collective-permute-done.4
  36.4 1.8 collective-permute-done.9
  38.7 37.4 %all_to_all.25 = bf16[8,4,16,1024]{3,2,1,0:T(8,128)(2,1)S(1)} all-to-all(bf16[8,4,16,1024]{3,2,1,0:T(8,128)(2,1)S(1)} %bitcast.79), channel_id=1, replica_groups={{0,2,4,6,8,10,12,14},{1,3,5,7,9,11,13,15},{16,18,20,22,24,26,28,30},{17..., dimensions={0} | all-to-all | bytes 2097152 | tf_op jit(solution)/shard_map/all_to_all | solution.py:42
  76.3 2.8 %collective-permute-start.12 = (bf16[16,1024]{1,0:T(8,128)(2,1)S(1)}, bf16[16,1024]{1,0:T(8,128)(2,1)S(1)}, u32[]{:S(2)}, u32[]{:S(2)}) collective-permute-start(bf16[16,1024]{1,0:T(8,128)(2,1)S(1)} %get-tuple-element.68), channel_id=1, source_target_pairs={{0,48},{16,0},{32,16},{48,32},{64,112},{80,64},{96,80},{112,96},{1... | collective-permute-start | bytes 98312 | tf_op jit(solution)/shard_map/ppermute | solution.py:33
  79.3 2.0 collective-permute-start.10
  81.2 3.2 %collective-permute-done.11 = bf16[16,1024]{1,0:T(8,128)(2,1)S(1)} collective-permute-done((bf16[16,1024]{1,0:T(8,128)(2,1)S(1)}, bf16[16,1024]{1,0:T(8,128)(2,1)S(1)}, u32[]{:S(2)}, u32[]{:S(2)}) %collective-permute-start.11) | collective-permute-done | bytes 32800 | tf_op jit(solution)/shard_map/ppermute | solution.py:33
  85.4 28.9 %all_to_all.26 = bf16[8,16,4096]{2,1,0:T(8,128)(2,1)S(1)} all-to-all(bf16[8,16,4096]{2,1,0:T(8,128)(2,1)S(1)} %broadcast_in_dim.56), channel_id=1, replica_groups={{0,2,4,6,8,10,12,14},{1,3,5,7,9,11,13,15},{16,18,20,22,24,26,28,30},{17..., dimensions={0} | all-to-all | bytes 2097152 | tf_op jit(solution)/shard_map/all_to_all | solution.py:42
  114.4 1.0 convolution_convert_fusion
  115.4 42.3 %all_to_all.27 = bf16[16,24,4096]{2,1,0:T(8,128)(2,1)S(1)} all-to-all(bf16[16,24,4096]{2,1,0:T(8,128)(2,1)S(1)} %bitcast.77), channel_id=1, replica_groups=mesh['expert'=16,'tensor'=16] {'expert'}, dimensions={0} | all-to-all | bytes 6291456 | tf_op jit(solution)/shard_map/all_to_all | solution.py:259
  157.6 10.5 %shard_map.110 = bf16[384,4096]{1,0:T(8,128)(2,1)S(1)} custom-call(bf16[384,4096]{1,0:T(8,128)(2,1)S(1)} %bitcast.73, bf16[4096,384]{1,0:T(8,128)(2,1)S(1)} %bitcast.76, bf16[4096,384]{1,0:T(8,128)(2,1)} %bitcast.3.up_a, bf16[4096,384]{1,0:T(8,128)(2,1)} %collective-permute-done.3.gate_b, bf16[4096,384]{1,0:T(8,128)(2,1)} %collective-permute-done.7.up_b, ...), custom_call_target="tpu_custom_call" | custom-call | flops 7247757312 | bytes 25165824 | tf_op jit(solution)/shard_map/pallas_call | solution.py:96
  168.1 36.8 %all_to_all.28 = bf16[16,24,4096]{2,1,0:T(8,128)(2,1)S(1)} all-to-all(bf16[16,24,4096]{2,1,0:T(8,128)(2,1)S(1)} %bitcast.74), channel_id=1, replica_groups=mesh['expert'=16,'tensor'=16] {'expert'}, dimensions={0} | all-to-all | bytes 6291456 | tf_op jit(solution)/shard_map/all_to_all | solution.py:266
  205.6 30.6 %all_to_all.29 = bf16[8,16,4096]{2,1,0:T(8,128)(2,1)S(1)} all-to-all(bf16[8,16,4096]{2,1,0:T(8,128)(2,1)S(1)} %bitcast.81), channel_id=1, replica_groups={{0,2,4,6,8,10,12,14},{1,3,5,7,9,11,13,15},{16,18,20,22,24,26,28,30},{17..., dimensions={0} | all-to-all | bytes 2097152 | tf_op jit(solution)/shard_map/all_to_all | solution.py:42
  (75 shorter events, 8.9 us)
Async XLA Ops:
  0.0 23.4 %copy-start.3 = (bf16[512,256]{1,0:T(8,128)(2,1)S(1)}, bf16[512,256]{1,0:T(8,128)(2,1)}, u32[]{:S(2)}) copy-start(bf16[512,256]{1,0:T(8,128)(2,1)} %param.14) | copy-start | bytes 786436
  0.0 17.8 %copy-start.6 = (bf16[256,8]{0,1:T(8,128)(2,1)S(1)}, bf16[256,8]{0,1:T(8,128)(2,1)}, u32[]{:S(2)}) copy-start(bf16[256,8]{0,1:T(8,128)(2,1)} %param.18) | copy-start | bytes 12292
  0.8 16.5 %collective-permute-start.3 = (bf16[4096,384]{1,0:T(8,128)(2,1)}, bf16[4096,384]{1,0:T(8,128)(2,1)}, u32[]{:S(2)}, u32[]{:S(2)}) collective-permute-start(bf16[4096,384]{1,0:T(8,128)(2,1)} %bitcast.75), channel_id=1, source_target_pairs={{0,1},{1,0},{2,3},{3,2},{4,5},{5,4},{6,7},{7,6},{8,9},{9,8},{10,11... | collective-permute-start | bytes 9437192 | tf_op jit(solution)/shard_map/ppermute | solution.py:24
  0.8 14.2 %collective-permute-start.1 = (bf16[512,256]{1,0:T(8,128)(2,1)}, bf16[512,256]{1,0:T(8,128)(2,1)S(1)}, u32[]{:S(2)}, u32[]{:S(2)}) collective-permute-start(bf16[512,256]{1,0:T(8,128)(2,1)} %param.14), channel_id=1, source_target_pairs={{0,128},{16,144},{32,160},{48,176},{64,192},{80,208},{96,224},{112... | collective-permute-start | bytes 786440 | tf_op jit(solution)/shard_map/ppermute | solution.py:33
  4.1 12.8 %collective-permute-start = (bf16[512,256]{1,0:T(8,128)(2,1)}, bf16[512,256]{1,0:T(8,128)(2,1)S(1)}, u32[]{:S(2)}, u32[]{:S(2)}) collective-permute-start(bf16[512,256]{1,0:T(8,128)(2,1)} %param.14), channel_id=1, source_target_pairs={{0,64},{16,80},{32,96},{48,112},{64,128},{80,144},{96,160},{112,17... | collective-permute-start | bytes 786440 | tf_op jit(solution)/shard_map/ppermute | solution.py:33
  4.8 12.5 %collective-permute-start.2 = (bf16[512,256]{1,0:T(8,128)(2,1)}, bf16[512,256]{1,0:T(8,128)(2,1)S(1)}, u32[]{:S(2)}, u32[]{:S(2)}) collective-permute-start(bf16[512,256]{1,0:T(8,128)(2,1)} %param.14), channel_id=1, source_target_pairs={{0,192},{16,208},{32,224},{48,240},{64,0},{80,16},{96,32},{112,48}... | collective-permute-start | bytes 786440 | tf_op jit(solution)/shard_map/ppermute | solution.py:33
  9.2 1.7 copy-start
  10.9 0.9 copy-start.1
  17.3 17.1 %collective-permute-start.7 = (bf16[4096,384]{1,0:T(8,128)(2,1)}, bf16[4096,384]{1,0:T(8,128)(2,1)}, u32[]{:S(2)}, u32[]{:S(2)}) collective-permute-start(bf16[4096,384]{1,0:T(8,128)(2,1)} %bitcast.3.up_a), channel_id=1, source_target_pairs={{0,1},{1,0},{2,3},{3,2},{4,5},{5,4},{6,7},{7,6},{8,9},{9,8},{10,11... | collective-permute-start | bytes 9437192 | tf_op jit(solution)/shard_map/ppermute | solution.py:24
  17.3 17.1 %collective-permute-start.8 = (bf16[384,4096]{1,0:T(8,128)(2,1)}, bf16[384,4096]{1,0:T(8,128)(2,1)}, u32[]{:S(2)}, u32[]{:S(2)}) collective-permute-start(bf16[384,4096]{1,0:T(8,128)(2,1)} %bitcast.4.down_a), channel_id=1, source_target_pairs={{0,1},{1,0},{2,3},{3,2},{4,5},{5,4},{6,7},{7,6},{8,9},{9,8},{10,11... | collective-permute-start | bytes 9437192 | tf_op jit(solution)/shard_map/ppermute | solution.py:24
  18.6 8.6 %collective-permute-start.6 = (bf16[2,8,16,512]{3,2,1,0:T(8,128)(2,1)S(1)}, bf16[2,8,16,512]{3,2,1,0:T(8,128)(2,1)S(1)}, u32[]{:S(2)}, u32[]{:S(2)}) collective-permute-start(bf16[2,8,16,512]{3,2,1,0:T(8,128)(2,1)S(1)} %shard_map.109), channel_id=1, source_target_pairs={{0,48},{16,0},{32,16},{48,32},{64,112},{80,64},{96,80},{112,96},{1... | collective-permute-start | bytes 786440 | tf_op jit(solution)/shard_map/ppermute | solution.py:33
  20.6 12.9 %collective-permute-start.5 = (bf16[2,8,16,512]{3,2,1,0:T(8,128)(2,1)S(1)}, bf16[2,8,16,512]{3,2,1,0:T(8,128)(2,1)S(1)}, u32[]{:S(2)}, u32[]{:S(2)}) collective-permute-start(bf16[2,8,16,512]{3,2,1,0:T(8,128)(2,1)S(1)} %shard_map.109), channel_id=1, source_target_pairs={{0,32},{16,48},{32,0},{48,16},{64,96},{80,112},{96,64},{112,80},{1... | collective-permute-start | bytes 786440 | tf_op jit(solution)/shard_map/ppermute | solution.py:33
  21.6 12.7 %collective-permute-start.4 = (bf16[2,8,16,512]{3,2,1,0:T(8,128)(2,1)S(1)}, bf16[2,8,16,512]{3,2,1,0:T(8,128)(2,1)S(1)}, u32[]{:S(2)}, u32[]{:S(2)}) collective-permute-start(bf16[2,8,16,512]{3,2,1,0:T(8,128)(2,1)S(1)} %shard_map.109), channel_id=1, source_target_pairs={{0,16},{16,32},{32,48},{48,0},{64,80},{80,96},{96,112},{112,64},{1... | collective-permute-start | bytes 786440 | tf_op jit(solution)/shard_map/ppermute | solution.py:33
  35.3 2.9 %collective-permute-start.9 = (bf16[512,1024]{1,0:T(8,128)(2,1)S(1)}, bf16[512,1024]{1,0:T(8,128)(2,1)S(1)}, u32[]{:S(2)}, u32[]{:S(2)}) collective-permute-start(bf16[512,1024]{1,0:T(8,128)(2,1)S(1)} %convolution_convert_fusion.2), channel_id=1, source_target_pairs={{0,1},{1,0},{2,3},{3,2},{4,5},{5,4},{6,7},{7,6},{8,9},{9,8},{10,11... | collective-permute-start | bytes 3145736 | tf_op jit(solution)/shard_map/ppermute | solution.py:24
  38.6 46.4 %copy-start.4 = (bf16[16,4096]{1,0:T(8,128)(2,1)S(1)}, bf16[16,4096]{1,0:T(8,128)(2,1)}, u32[]{:S(2)}) copy-start(bf16[16,4096]{1,0:T(8,128)(2,1)} %param.15) | copy-start | bytes 393220
  38.6 46.6 %copy-start.5 = (f32[4096]{0:T(1024)S(1)}, f32[4096]{0:T(1024)}, u32[]{:S(2)}) copy-start(f32[4096]{0:T(1024)} %param.16) | copy-start | bytes 49156
  76.3 4.9 %collective-permute-start.12 = (bf16[16,1024]{1,0:T(8,128)(2,1)S(1)}, bf16[16,1024]{1,0:T(8,128)(2,1)S(1)}, u32[]{:S(2)}, u32[]{:S(2)}) collective-permute-start(bf16[16,1024]{1,0:T(8,128)(2,1)S(1)} %get-tuple-element.68), channel_id=1, source_target_pairs={{0,48},{16,0},{32,16},{48,32},{64,112},{80,64},{96,80},{112,96},{1... | collective-permute-start | bytes 98312 | tf_op jit(solution)/shard_map/ppermute | solution.py:33
  79.1 5.4 %collective-permute-start.11 = (bf16[16,1024]{1,0:T(8,128)(2,1)S(1)}, bf16[16,1024]{1,0:T(8,128)(2,1)S(1)}, u32[]{:S(2)}, u32[]{:S(2)}) collective-permute-start(bf16[16,1024]{1,0:T(8,128)(2,1)S(1)} %get-tuple-element.69), channel_id=1, source_target_pairs={{0,32},{16,48},{32,0},{48,16},{64,96},{80,112},{96,64},{112,80},{1... | collective-permute-start | bytes 98312 | tf_op jit(solution)/shard_map/ppermute | solution.py:33
  79.3 5.3 %collective-permute-start.10 = (bf16[16,1024]{1,0:T(8,128)(2,1)S(1)}, bf16[16,1024]{1,0:T(8,128)(2,1)S(1)}, u32[]{:S(2)}, u32[]{:S(2)}) collective-permute-start(bf16[16,1024]{1,0:T(8,128)(2,1)S(1)} %get-tuple-element.70), channel_id=1, source_target_pairs={{0,16},{16,32},{32,48},{48,0},{64,80},{80,96},{96,112},{112,64},{1... | collective-permute-start | bytes 98312 | tf_op jit(solution)/shard_map/ppermute | solution.py:33
  115.3 42.3 %copy-start.2 = (bf16[1,4096,384]{2,1,0:T(8,128)(2,1)S(1)}, bf16[1,4096,384]{2,1,0:T(8,128)(2,1)}, u32[]{:S(2)}) copy-start(bf16[1,4096,384]{2,1,0:T(8,128)(2,1)} %param.19) | copy-start | bytes 9437188
